TPU v7x, 1024 devices: a whole 8x8x8 slice. The times are simulated.
1024 devices in a mesh: mem: 16 (over z, x_lo), rows: 64 (over y, x_hi, core).
Axes of the slice: x: 8 (x_hi: 4, x_lo: 2; x = x_hi * 2 + x_lo), y: 8, z: 8, core: 2. Of those that a mesh axis runs over, the one named last changes fastest.
Arguments:
- sample_collection: float32 [256, 2, 512, 128], P('mem', None, 'rows'), may hold values from -6 to 6
- obs_values: float32 [2, 512, 128], P(None, 'rows', 'mem'), may hold values from -6 to 6
- obs_inverse_variance: float32 [2, 512, 128], P(None, 'rows', 'mem'), may hold values from 0.5 to 4
- obs_mask: int32 [2, 512, 128], P(None, 'rows', 'mem'), may hold values 0 or 1
Outputs:
- cycled: float32 [256, 2, 512, 128], P('mem', None, 'rows')
All inputs are finite; a program needn't handle non-finite values. No bound on the sum of `obs_mask` on one device may be relied on, other than what follows from the above.
Results may differ from a plain program's by a relative error of at most 0.0051.
Values may be sent and summed in bfloat16 or wider, within the bound.
A program may use at most 32 MiB of HBM per device.

v0:
```python
import jax
import jax.numpy as jnp
from jax import lax
from jax.sharding import PartitionSpec as P

PATCH = 8
RADIUS = 4
FSTEPS = 4
SCHULZ_STEPS = 3


CADV = 0.05


def with_halo(shard, sides, width):
    for axis, dim in sides:
        count, length = (lax.axis_size(axis), shard.shape[dim])
        up = [(i, (i + 1) % count) for i in range(count)]
        down = [(j, i) for i, j in up]
        last = lax.slice_in_dim(shard, length - width, length, axis=dim)
        initial = lax.slice_in_dim(shard, 0, width, axis=dim)
        before = lax.ppermute(last, axis, up)
        after = lax.ppermute(initial, axis, down)
        shard = jnp.concatenate([before, shard, after], axis=dim)
    return shard


def advance_rows(extended):
    u_field = extended[:, 0]
    v_field = extended[:, 1]

    def tendency(field):
        along_x = jnp.roll(field, -1, -1) - jnp.roll(field, 1, -1)
        along_y = field[:, 2:] - field[:, :-2]
        return field[:, 1:-1] - CADV * (
            u_field[:, 1:-1] * along_x[:, 1:-1] + v_field[:, 1:-1] * along_y
        )

    return jnp.stack([tendency(u_field), tendency(v_field)], 1)


def predicted_prior(dynamics_fields):
    for step in range(FSTEPS):
        extended = with_halo(dynamics_fields, (("rows", 2),), 1)
        dynamics_fields = advance_rows(extended)
    return dynamics_fields


def owner_layout(fields):
    local_members, fields_count, band_rows, complete_width = fields.shape
    owning_patches = lax.axis_size("mem")
    col_width = complete_width // owning_patches
    split = fields.reshape(local_members, fields_count, band_rows, owning_patches, col_width)
    split = jnp.transpose(split, (0, 3, 1, 2, 4))
    return split.reshape(local_members, owning_patches, fields_count * band_rows * col_width)


def taper_table():
    index = jnp.arange(2 * PATCH)
    dist = jnp.maximum(jnp.maximum(RADIUS - index, index - (RADIUS + PATCH - 1)), 0)
    far = jnp.maximum(dist[:, None], dist[None, :]).astype(jnp.float32)
    return 1.0 - far / (RADIUS + 1.0)


def analyse(dev_ext, obs_ext, mean):
    high = lax.Precision.HIGHEST
    members = dev_ext.shape[-1]
    col_width = dev_ext.shape[2] - 2 * RADIUS
    count = col_width // PATCH
    taper = taper_table()[None, :, :]
    factor = obs_ext[..., 0].astype(jnp.float32) * taper
    weighted = (dev_ext.astype(jnp.float32) * factor[..., None]).astype(jnp.bfloat16)
    weighted_list = [weighted.reshape(-1, members)]
    region_list = [dev_ext.reshape(-1, members)]
    innov_list = [obs_ext[..., 1].reshape(-1)]
    inner = dev_ext[:, RADIUS : RADIUS + PATCH, RADIUS : RADIUS + PATCH, :]
    interior_pieces = [inner.reshape(-1, members)]
    weighted_all = jnp.stack(weighted_list)
    region_all = jnp.stack(region_list)
    innovation_combined = jnp.stack(innov_list)
    interior_combined = jnp.stack(interior_pieces)
    gram = jnp.einsum("pqk,pql->pkl", weighted_all, region_all, preferred_element_type=jnp.float32)
    projected = jnp.einsum(
        "pqk,pq->pk",
        weighted_all.astype(jnp.float32),
        innovation_combined.astype(jnp.float32),
        precision=high,
    )
    eye = jnp.eye(members, dtype=jnp.float32)
    system = (members - 1.0) * eye + gram
    scale = jnp.sqrt(jnp.sum(system * system, axis=(1, 2)))[:, None, None]
    iter_y = system / scale
    iter_z = jnp.broadcast_to(eye, system.shape)
    for step in range(SCHULZ_STEPS):
        middle = 1.5 * eye - 0.5 * jnp.matmul(iter_z, iter_y, precision=high)
        iter_y = jnp.matmul(iter_y, middle, precision=high)
        iter_z = jnp.matmul(middle, iter_z, precision=high)
    root = iter_z / jnp.sqrt(scale)
    half_way = jnp.einsum("pkl,pl->pk", root, projected, precision=high)
    shift = jnp.einsum("pkl,pl->pk", root, half_way, precision=high)
    ensemble_transform = (jnp.sqrt(members - 1.0) * root + shift[:, :, None]).astype(jnp.bfloat16)
    increment = jnp.einsum(
        "vhf,vfa->vha", interior_combined, ensemble_transform, preferred_element_type=jnp.float32
    )
    increment = increment.reshape(count, 2, PATCH, PATCH, members)
    increment = jnp.transpose(increment, (1, 2, 0, 3, 4)).reshape(2, PATCH, col_width, members)
    return mean[..., None] + increment


def local(sample_collection, obs_values, obs_inverse_variance, obs_mask):
    leading_output = predicted_prior(sample_collection)
    local_members, fields_count, band_rows, complete_width = leading_output.shape
    col_width = obs_values.shape[2]
    owning_patches = lax.axis_size("mem")
    members = local_members * owning_patches
    sending = owner_layout(leading_output)
    gathered = lax.all_to_all(sending, "mem", split_axis=1, concat_axis=0, tiled=True)
    gathered = gathered.reshape(members, -1)
    mean_flat = jnp.sum(gathered, 0) / members
    deviation_flat = (gathered - mean_flat).astype(jnp.bfloat16)
    mean = mean_flat.reshape(fields_count, band_rows, col_width)
    deviation = jnp.transpose(deviation_flat).reshape(fields_count, band_rows, col_width, members)
    member_weight = (obs_mask.astype(jnp.float32) * obs_inverse_variance).astype(jnp.bfloat16)
    innovation = (obs_values - mean).astype(jnp.bfloat16)
    obs_pair = jnp.stack([member_weight, innovation], -1)
    dev_ext, obs_ext = (
        with_halo(deviation, (("rows", 1), ("mem", 2)), RADIUS),
        with_halo(obs_pair, (("rows", 1), ("mem", 2)), RADIUS),
    )
    updated_estimate = analyse(dev_ext, obs_ext, mean)
    returning = jnp.transpose(updated_estimate.reshape(-1, members)).reshape(members, 1, -1)
    output_result = lax.all_to_all(returning, "mem", split_axis=0, concat_axis=1, tiled=True)
    output_result = output_result.reshape(
        local_members, owning_patches, fields_count, band_rows, col_width
    )
    output_result = jnp.transpose(output_result, (0, 2, 3, 1, 4)).reshape(
        local_members, fields_count, band_rows, complete_width
    )
    return predicted_prior(output_result)


def solution(mesh):
    return jax.shard_map(
        local,
        mesh=mesh,
        in_specs=(
            P("mem", None, "rows", None),
            P(None, "rows", "mem"),
            P(None, "rows", "mem"),
            P(None, "rows", "mem"),
        ),
        out_specs=P("mem", None, "rows", None),
        check_vma=False,
    )
```

profile of v0, /device:TPU:61, one launch (start us, length us, event | category | flops | bytes accessed | tf_op | source)
XLA Modules:
  0.0 208.0 jit_solution(11822519058559427511)
XLA Ops:
  0.0 1.2 copy.175
  1.3 4.9 %collective-permute-start = (f32[16,2,1,128]{0,3,2,1:T(8,128)S(1)}, f32[16,2,1,128]{0,3,2,1:T(8,128)S(1)}, u32[]{:S(2)}, u32[]{:S(2)}) collective-permute-start(f32[16,2,1,128]{0,3,2,1:T(8,128)S(1)} %get-tuple-element.51), channel_id=1, source_target_pairs={{0,1},{1,2},{2,3},{3,4},{4,5},{5,6},{6,7},{7,8},{8,9},{9,10},{10,1... | collective-permute-start | bytes 49160 | tf_op jit(solution)/shard_map/ppermute | solution.py:22
  6.2 1.9 collective-permute-start.1
  8.1 10.0 %collective-permute-done.1 = f32[16,2,1,128]{0,3,2,1:T(8,128)S(1)} collective-permute-done((f32[16,2,1,128]{0,3,2,1:T(8,128)S(1)}, f32[16,2,1,128]{0,3,2,1:T(8,128)S(1)}, u32[]{:S(2)}, u32[]{:S(2)}) %collective-permute-start.1) | collective-permute-done | bytes 16416 | tf_op jit(solution)/shard_map/ppermute | solution.py:23
  18.4 0.3 fusion.160
  18.7 0.4 fusion.113
  19.2 1.9 collective-permute-start.2
  21.1 2.4 %collective-permute-start.3 = (f32[16,2,1,128]{0,3,2,1:T(8,128)S(1)}, f32[16,2,1,128]{0,3,2,1:T(8,128)S(1)}, u32[]{:S(2)}, u32[]{:S(2)}) collective-permute-start(f32[16,2,1,128]{0,3,2,1:T(8,128)S(1)} %get-tuple-element.50), channel_id=1, source_target_pairs={{1,0},{2,1},{3,2},{4,3},{5,4},{6,5},{7,6},{8,7},{9,8},{10,9},{11,1... | collective-permute-start | bytes 49160 | tf_op jit(solution)/shard_map/ppermute | solution.py:23
  23.5 9.4 %collective-permute-done.3 = f32[16,2,1,128]{0,3,2,1:T(8,128)S(1)} collective-permute-done((f32[16,2,1,128]{0,3,2,1:T(8,128)S(1)}, f32[16,2,1,128]{0,3,2,1:T(8,128)S(1)}, u32[]{:S(2)}, u32[]{:S(2)}) %collective-permute-start.3) | collective-permute-done | bytes 16416 | tf_op jit(solution)/shard_map/ppermute | solution.py:23
  33.4 0.4 fusion.99
  33.9 1.9 collective-permute-start.4
  35.8 2.4 %collective-permute-start.5 = (f32[16,2,1,128]{0,3,2,1:T(8,128)S(1)}, f32[16,2,1,128]{0,3,2,1:T(8,128)S(1)}, u32[]{:S(2)}, u32[]{:S(2)}) collective-permute-start(f32[16,2,1,128]{0,3,2,1:T(8,128)S(1)} %get-tuple-element.48), channel_id=1, source_target_pairs={{1,0},{2,1},{3,2},{4,3},{5,4},{6,5},{7,6},{8,7},{9,8},{10,9},{11,1... | collective-permute-start | bytes 49160 | tf_op jit(solution)/shard_map/ppermute | solution.py:23
  38.2 8.2 %collective-permute-done.5 = f32[16,2,1,128]{0,3,2,1:T(8,128)S(1)} collective-permute-done((f32[16,2,1,128]{0,3,2,1:T(8,128)S(1)}, f32[16,2,1,128]{0,3,2,1:T(8,128)S(1)}, u32[]{:S(2)}, u32[]{:S(2)}) %collective-permute-start.5) | collective-permute-done | bytes 16416 | tf_op jit(solution)/shard_map/ppermute | solution.py:23
  46.9 0.4 fusion.85
  47.4 1.9 collective-permute-start.6
  49.3 2.4 %collective-permute-start.7 = (f32[16,2,1,128]{0,3,2,1:T(8,128)S(1)}, f32[16,2,1,128]{0,3,2,1:T(8,128)S(1)}, u32[]{:S(2)}, u32[]{:S(2)}) collective-permute-start(f32[16,2,1,128]{0,3,2,1:T(8,128)S(1)} %get-tuple-element.46), channel_id=1, source_target_pairs={{1,0},{2,1},{3,2},{4,3},{5,4},{6,5},{7,6},{8,7},{9,8},{10,9},{11,1... | collective-permute-start | bytes 49160 | tf_op jit(solution)/shard_map/ppermute | solution.py:23
  51.7 8.1 %collective-permute-done.7 = f32[16,2,1,128]{0,3,2,1:T(8,128)S(1)} collective-permute-done((f32[16,2,1,128]{0,3,2,1:T(8,128)S(1)}, f32[16,2,1,128]{0,3,2,1:T(8,128)S(1)}, u32[]{:S(2)}, u32[]{:S(2)}) %collective-permute-start.7) | collective-permute-done | bytes 16416 | tf_op jit(solution)/shard_map/ppermute | solution.py:23
  60.3 0.4 fusion.71
  60.9 0.9 copy.178
  61.8 1.0 copy.179
  62.8 16.5 %all-to-all-start = ((f32[16,16,128]{2,0,1:T(8,128)}), f32[16,16,128]{2,0,1:T(8,128)S(1)}, u32[]{:S(2)}, u32[]{:S(2)}) async-start(f32[16,16,128]{2,0,1:T(8,128)} %copy.179), calls=%async_computation | async-start | bytes 262144 | tf_op jit(solution)/shard_map/all_to_all | solution.py:117
  79.4 7.8 %all-to-all-done = f32[16,16,128]{2,0,1:T(8,128)S(1)} async-done(((f32[16,16,128]{2,0,1:T(8,128)}), f32[16,16,128]{2,0,1:T(8,128)S(1)}, u32[]{:S(2)}, u32[]{:S(2)}) %all-to-all-start) | async-done | bytes 131104 | tf_op jit(solution)/shard_map/all_to_all | solution.py:117
  87.4 3.2 %collective-permute-start.12 = (bf16[2,4,8,2]{2,1,0,3:T(4,128)(2,1)S(1)}, bf16[2,4,8,2]{2,1,0,3:T(4,128)(2,1)S(1)}, u32[]{:S(2)}, u32[]{:S(2)}) collective-permute-start(bf16[2,4,8,2]{2,1,0,3:T(4,128)(2,1)S(1)} %get-tuple-element.123), channel_id=1, source_target_pairs={{0,1},{1,2},{2,3},{3,4},{4,5},{5,6},{6,7},{7,8},{8,9},{9,10},{10,1... | collective-permute-start | bytes 776 | tf_op jit(solution)/shard_map/ppermute | solution.py:22
  90.6 1.9 collective-permute-start.13
  92.7 7.1 %collective-permute-done.13 = bf16[2,4,8,2]{2,1,0,3:T(4,128)(2,1)S(1)} collective-permute-done((bf16[2,4,8,2]{2,1,0,3:T(4,128)(2,1)S(1)}, bf16[2,4,8,2]{2,1,0,3:T(4,128)(2,1)S(1)}, u32[]{:S(2)}, u32[]{:S(2)}) %collective-permute-start.13) | collective-permute-done | bytes 288 | tf_op jit(solution)/shard_map/ppermute | solution.py:23
  99.9 2.9 %collective-permute-start.14 = (bf16[2,16,4,2]{2,1,0,3:T(8,128)(2,1)S(1)}, bf16[2,16,4,2]{2,1,0,3:T(8,128)(2,1)S(1)}, u32[]{:S(2)}, u32[]{:S(2)}) collective-permute-start(bf16[2,16,4,2]{2,1,0,3:T(8,128)(2,1)S(1)} %get-tuple-element.121), channel_id=1, source_target_pairs={{0,64},{64,128},{128,192},{192,256},{256,320},{320,384},{384,448},... | collective-permute-start | bytes 1544 | tf_op jit(solution)/shard_map/ppermute | solution.py:22
  102.8 4.5 %collective-permute-start.15 = (bf16[2,16,4,2]{2,1,0,3:T(8,128)(2,1)S(1)}, bf16[2,16,4,2]{2,1,0,3:T(8,128)(2,1)S(1)}, u32[]{:S(2)}, u32[]{:S(2)}) collective-permute-start(bf16[2,16,4,2]{2,1,0,3:T(8,128)(2,1)S(1)} %get-tuple-element.122), channel_id=1, source_target_pairs={{64,0},{128,64},{192,128},{256,192},{320,256},{384,320},{448,384},... | collective-permute-start | bytes 1544 | tf_op jit(solution)/shard_map/ppermute | solution.py:23
  107.3 2.5 %collective-permute-start.8 = (bf16[2,4,8,256]{3,2,1,0:T(8,128)(2,1)S(1)}, bf16[2,4,8,256]{3,2,1,0:T(8,128)(2,1)S(1)}, u32[]{:S(2)}, u32[]{:S(2)}) collective-permute-start(bf16[2,4,8,256]{3,2,1,0:T(8,128)(2,1)S(1)} %get-tuple-element.119), channel_id=1, source_target_pairs={{0,1},{1,2},{2,3},{3,4},{4,5},{5,6},{6,7},{7,8},{8,9},{9,10},{10,1... | collective-permute-start | bytes 98312 | tf_op jit(solution)/shard_map/ppermute | solution.py:22
  109.8 1.9 collective-permute-start.9
  111.8 7.4 %collective-permute-done.9 = bf16[2,4,8,256]{3,2,1,0:T(8,128)(2,1)S(1)} collective-permute-done((bf16[2,4,8,256]{3,2,1,0:T(8,128)(2,1)S(1)}, bf16[2,4,8,256]{3,2,1,0:T(8,128)(2,1)S(1)}, u32[]{:S(2)}, u32[]{:S(2)}) %collective-permute-start.9) | collective-permute-done | bytes 32800 | tf_op jit(solution)/shard_map/ppermute | solution.py:23
  119.3 1.9 collective-permute-start.10
  121.3 5.5 %collective-permute-start.11 = (bf16[2,16,4,256]{3,2,1,0:T(4,128)(2,1)S(1)}, bf16[2,16,4,256]{3,2,1,0:T(4,128)(2,1)S(1)}, u32[]{:S(2)}, u32[]{:S(2)}) collective-permute-start(bf16[2,16,4,256]{3,2,1,0:T(4,128)(2,1)S(1)} %get-tuple-element.118), channel_id=1, source_target_pairs={{64,0},{128,64},{192,128},{256,192},{320,256},{384,320},{448,384},... | collective-permute-start | bytes 196616 | tf_op jit(solution)/shard_map/ppermute | solution.py:23
  126.9 1.2 collective-permute-done.11
  128.1 1.1 multiply_reduce_fusion
  129.8 0.3 fusion.2
  130.1 0.4 fusion.122
  130.5 0.3 fusion.116
  130.8 0.4 fusion.1
  131.2 0.4 fusion.167
  131.6 0.4 fusion.166
  132.3 0.4 fusion
  132.7 0.4 convolution_divide_fusion
  133.4 0.3 fusion.168
  133.7 0.3 convolution_add_fusion
  134.1 13.0 %all_to_all.30 = f32[256,1,128]{2,1,0:T(1,128)S(1)} all-to-all(f32[256,1,128]{2,1,0:T(1,128)S(1)} %bitcast.148), channel_id=1, replica_groups=mesh['mem'=16,'rows'=64] {'mem'}, dimensions={0} | all-to-all | bytes 262144 | tf_op jit(solution)/shard_map/all_to_all | solution.py:132
  147.1 0.3 copy.182
  147.5 0.7 copy.183
  148.2 4.8 %collective-permute-start.16 = (f32[16,2,1,128]{0,3,2,1:T(8,128)S(1)}, f32[16,2,1,128]{0,3,2,1:T(8,128)S(1)}, u32[]{:S(2)}, u32[]{:S(2)}) collective-permute-start(f32[16,2,1,128]{0,3,2,1:T(8,128)S(1)} %get-tuple-element.43), channel_id=1, source_target_pairs={{0,1},{1,2},{2,3},{3,4},{4,5},{5,6},{6,7},{7,8},{8,9},{9,10},{10,1... | collective-permute-start | bytes 49160 | tf_op jit(solution)/shard_map/ppermute | solution.py:22
  153.0 2.1 %collective-permute-start.17 = (f32[16,2,1,128]{0,3,2,1:T(8,128)S(1)}, f32[16,2,1,128]{0,3,2,1:T(8,128)S(1)}, u32[]{:S(2)}, u32[]{:S(2)}) collective-permute-start(f32[16,2,1,128]{0,3,2,1:T(8,128)S(1)} %get-tuple-element.44), channel_id=1, source_target_pairs={{1,0},{2,1},{3,2},{4,3},{5,4},{6,5},{7,6},{8,7},{9,8},{10,9},{11,1... | collective-permute-start | bytes 49160 | tf_op jit(solution)/shard_map/ppermute | solution.py:23
  155.1 9.9 %collective-permute-done.17 = f32[16,2,1,128]{0,3,2,1:T(8,128)S(1)} collective-permute-done((f32[16,2,1,128]{0,3,2,1:T(8,128)S(1)}, f32[16,2,1,128]{0,3,2,1:T(8,128)S(1)}, u32[]{:S(2)}, u32[]{:S(2)}) %collective-permute-start.17) | collective-permute-done | bytes 16416 | tf_op jit(solution)/shard_map/ppermute | solution.py:23
  165.5 0.4 fusion.57
  166.0 1.9 collective-permute-start.18
  167.9 2.4 %collective-permute-start.19 = (f32[16,2,1,128]{0,3,2,1:T(8,128)S(1)}, f32[16,2,1,128]{0,3,2,1:T(8,128)S(1)}, u32[]{:S(2)}, u32[]{:S(2)}) collective-permute-start(f32[16,2,1,128]{0,3,2,1:T(8,128)S(1)} %get-tuple-element.42), channel_id=1, source_target_pairs={{1,0},{2,1},{3,2},{4,3},{5,4},{6,5},{7,6},{8,7},{9,8},{10,9},{11,1... | collective-permute-start | bytes 49160 | tf_op jit(solution)/shard_map/ppermute | solution.py:23
  170.3 8.8 %collective-permute-done.19 = f32[16,2,1,128]{0,3,2,1:T(8,128)S(1)} collective-permute-done((f32[16,2,1,128]{0,3,2,1:T(8,128)S(1)}, f32[16,2,1,128]{0,3,2,1:T(8,128)S(1)}, u32[]{:S(2)}, u32[]{:S(2)}) %collective-permute-start.19) | collective-permute-done | bytes 16416 | tf_op jit(solution)/shard_map/ppermute | solution.py:23
  179.6 0.4 fusion.43
  180.1 1.9 collective-permute-start.20
  182.0 2.4 %collective-permute-start.21 = (f32[16,2,1,128]{0,3,2,1:T(8,128)S(1)}, f32[16,2,1,128]{0,3,2,1:T(8,128)S(1)}, u32[]{:S(2)}, u32[]{:S(2)}) collective-permute-start(f32[16,2,1,128]{0,3,2,1:T(8,128)S(1)} %get-tuple-element.40), channel_id=1, source_target_pairs={{1,0},{2,1},{3,2},{4,3},{5,4},{6,5},{7,6},{8,7},{9,8},{10,9},{11,1... | collective-permute-start | bytes 49160 | tf_op jit(solution)/shard_map/ppermute | solution.py:23
  184.5 8.2 %collective-permute-done.21 = f32[16,2,1,128]{0,3,2,1:T(8,128)S(1)} collective-permute-done((f32[16,2,1,128]{0,3,2,1:T(8,128)S(1)}, f32[16,2,1,128]{0,3,2,1:T(8,128)S(1)}, u32[]{:S(2)}, u32[]{:S(2)}) %collective-permute-start.21) | collective-permute-done | bytes 16416 | tf_op jit(solution)/shard_map/ppermute | solution.py:23
  193.1 0.4 fusion.29
  193.6 1.9 collective-permute-start.22
  195.5 2.4 %collective-permute-start.23 = (f32[16,2,1,128]{0,3,2,1:T(8,128)S(1)}, f32[16,2,1,128]{0,3,2,1:T(8,128)S(1)}, u32[]{:S(2)}, u32[]{:S(2)}) collective-permute-start(f32[16,2,1,128]{0,3,2,1:T(8,128)S(1)} %get-tuple-element.38), channel_id=1, source_target_pairs={{1,0},{2,1},{3,2},{4,3},{5,4},{6,5},{7,6},{8,7},{9,8},{10,9},{11,1... | collective-permute-start | bytes 49160 | tf_op jit(solution)/shard_map/ppermute | solution.py:23
  197.9 8.1 %collective-permute-done.23 = f32[16,2,1,128]{0,3,2,1:T(8,128)S(1)} collective-permute-done((f32[16,2,1,128]{0,3,2,1:T(8,128)S(1)}, f32[16,2,1,128]{0,3,2,1:T(8,128)S(1)}, u32[]{:S(2)}, u32[]{:S(2)}) %collective-permute-start.23) | collective-permute-done | bytes 16416 | tf_op jit(solution)/shard_map/ppermute | solution.py:23
  206.5 0.4 fusion.15
  207.3 0.7 pad_maximum_fusion.54
  (98 shorter events, 5.6 us)
Async XLA Ops:
  1.3 6.9 %collective-permute-start = (f32[16,2,1,128]{0,3,2,1:T(8,128)S(1)}, f32[16,2,1,128]{0,3,2,1:T(8,128)S(1)}, u32[]{:S(2)}, u32[]{:S(2)}) collective-permute-start(f32[16,2,1,128]{0,3,2,1:T(8,128)S(1)} %get-tuple-element.51), channel_id=1, source_target_pairs={{0,1},{1,2},{2,3},{3,4},{4,5},{5,6},{6,7},{7,8},{8,9},{9,10},{10,1... | collective-permute-start | bytes 49160 | tf_op jit(solution)/shard_map/ppermute | solution.py:22
  6.2 11.9 %collective-permute-start.1 = (f32[16,2,1,128]{0,3,2,1:T(8,128)S(1)}, f32[16,2,1,128]{0,3,2,1:T(8,128)S(1)}, u32[]{:S(2)}, u32[]{:S(2)}) collective-permute-start(f32[16,2,1,128]{0,3,2,1:T(8,128)S(1)} %get-tuple-element.52), channel_id=1, source_target_pairs={{1,0},{2,1},{3,2},{4,3},{5,4},{6,5},{7,6},{8,7},{9,8},{10,9},{11,1... | collective-permute-start | bytes 49160 | tf_op jit(solution)/shard_map/ppermute | solution.py:23
  19.2 4.3 %collective-permute-start.2 = (f32[16,2,1,128]{0,3,2,1:T(8,128)S(1)}, f32[16,2,1,128]{0,3,2,1:T(8,128)S(1)}, u32[]{:S(2)}, u32[]{:S(2)}) collective-permute-start(f32[16,2,1,128]{0,3,2,1:T(8,128)S(1)} %get-tuple-element.49), channel_id=1, source_target_pairs={{0,1},{1,2},{2,3},{3,4},{4,5},{5,6},{6,7},{7,8},{8,9},{9,10},{10,1... | collective-permute-start | bytes 49160 | tf_op jit(solution)/shard_map/ppermute | solution.py:22
  21.1 11.8 %collective-permute-start.3 = (f32[16,2,1,128]{0,3,2,1:T(8,128)S(1)}, f32[16,2,1,128]{0,3,2,1:T(8,128)S(1)}, u32[]{:S(2)}, u32[]{:S(2)}) collective-permute-start(f32[16,2,1,128]{0,3,2,1:T(8,128)S(1)} %get-tuple-element.50), channel_id=1, source_target_pairs={{1,0},{2,1},{3,2},{4,3},{5,4},{6,5},{7,6},{8,7},{9,8},{10,9},{11,1... | collective-permute-start | bytes 49160 | tf_op jit(solution)/shard_map/ppermute | solution.py:23
  33.9 4.3 %collective-permute-start.4 = (f32[16,2,1,128]{0,3,2,1:T(8,128)S(1)}, f32[16,2,1,128]{0,3,2,1:T(8,128)S(1)}, u32[]{:S(2)}, u32[]{:S(2)}) collective-permute-start(f32[16,2,1,128]{0,3,2,1:T(8,128)S(1)} %get-tuple-element.47), channel_id=1, source_target_pairs={{0,1},{1,2},{2,3},{3,4},{4,5},{5,6},{6,7},{7,8},{8,9},{9,10},{10,1... | collective-permute-start | bytes 49160 | tf_op jit(solution)/shard_map/ppermute | solution.py:22
  35.8 10.6 %collective-permute-start.5 = (f32[16,2,1,128]{0,3,2,1:T(8,128)S(1)}, f32[16,2,1,128]{0,3,2,1:T(8,128)S(1)}, u32[]{:S(2)}, u32[]{:S(2)}) collective-permute-start(f32[16,2,1,128]{0,3,2,1:T(8,128)S(1)} %get-tuple-element.48), channel_id=1, source_target_pairs={{1,0},{2,1},{3,2},{4,3},{5,4},{6,5},{7,6},{8,7},{9,8},{10,9},{11,1... | collective-permute-start | bytes 49160 | tf_op jit(solution)/shard_map/ppermute | solution.py:23
  47.4 4.4 %collective-permute-start.6 = (f32[16,2,1,128]{0,3,2,1:T(8,128)S(1)}, f32[16,2,1,128]{0,3,2,1:T(8,128)S(1)}, u32[]{:S(2)}, u32[]{:S(2)}) collective-permute-start(f32[16,2,1,128]{0,3,2,1:T(8,128)S(1)} %get-tuple-element.45), channel_id=1, source_target_pairs={{0,1},{1,2},{2,3},{3,4},{4,5},{5,6},{6,7},{7,8},{8,9},{9,10},{10,1... | collective-permute-start | bytes 49160 | tf_op jit(solution)/shard_map/ppermute | solution.py:22
  49.3 10.5 %collective-permute-start.7 = (f32[16,2,1,128]{0,3,2,1:T(8,128)S(1)}, f32[16,2,1,128]{0,3,2,1:T(8,128)S(1)}, u32[]{:S(2)}, u32[]{:S(2)}) collective-permute-start(f32[16,2,1,128]{0,3,2,1:T(8,128)S(1)} %get-tuple-element.46), channel_id=1, source_target_pairs={{1,0},{2,1},{3,2},{4,3},{5,4},{6,5},{7,6},{8,7},{9,8},{10,9},{11,1... | collective-permute-start | bytes 49160 | tf_op jit(solution)/shard_map/ppermute | solution.py:23
  60.8 18.5 %copy-start = (f32[2,8,8]{2,1,0:T(8,128)S(1)}, f32[2,8,8]{2,1,0:T(8,128)}, u32[]{:S(2)}) copy-start(f32[2,8,8]{2,1,0:T(8,128)} %param.6) | copy-start | bytes 1540
  60.8 18.5 %copy-start.1 = (s32[2,8,8]{2,1,0:T(8,128)S(1)}, s32[2,8,8]{2,1,0:T(8,128)}, u32[]{:S(2)}) copy-start(s32[2,8,8]{2,1,0:T(8,128)} %param.7) | copy-start | bytes 1540
  61.8 25.6 %copy-start.2 = (f32[2,8,8]{2,1,0:T(8,128)S(1)}, f32[2,8,8]{2,1,0:T(8,128)}, u32[]{:S(2)}) copy-start(f32[2,8,8]{2,1,0:T(8,128)} %param.5) | copy-start | bytes 1540
  62.8 24.5 %all-to-all-start = ((f32[16,16,128]{2,0,1:T(8,128)}), f32[16,16,128]{2,0,1:T(8,128)S(1)}, u32[]{:S(2)}, u32[]{:S(2)}) async-start(f32[16,16,128]{2,0,1:T(8,128)} %copy.179), calls=%async_computation | async-start | bytes 262144 | tf_op jit(solution)/shard_map/all_to_all | solution.py:117
  87.4 5.3 %collective-permute-start.12 = (bf16[2,4,8,2]{2,1,0,3:T(4,128)(2,1)S(1)}, bf16[2,4,8,2]{2,1,0,3:T(4,128)(2,1)S(1)}, u32[]{:S(2)}, u32[]{:S(2)}) collective-permute-start(bf16[2,4,8,2]{2,1,0,3:T(4,128)(2,1)S(1)} %get-tuple-element.123), channel_id=1, source_target_pairs={{0,1},{1,2},{2,3},{3,4},{4,5},{5,6},{6,7},{7,8},{8,9},{9,10},{10,1... | collective-permute-start | bytes 776 | tf_op jit(solution)/shard_map/ppermute | solution.py:22
  90.6 9.1 %collective-permute-start.13 = (bf16[2,4,8,2]{2,1,0,3:T(4,128)(2,1)S(1)}, bf16[2,4,8,2]{2,1,0,3:T(4,128)(2,1)S(1)}, u32[]{:S(2)}, u32[]{:S(2)}) collective-permute-start(bf16[2,4,8,2]{2,1,0,3:T(4,128)(2,1)S(1)} %get-tuple-element.124), channel_id=1, source_target_pairs={{1,0},{2,1},{3,2},{4,3},{5,4},{6,5},{7,6},{8,7},{9,8},{10,9},{11,1... | collective-permute-start | bytes 776 | tf_op jit(solution)/shard_map/ppermute | solution.py:23
  99.9 11.9 %collective-permute-start.14 = (bf16[2,16,4,2]{2,1,0,3:T(8,128)(2,1)S(1)}, bf16[2,16,4,2]{2,1,0,3:T(8,128)(2,1)S(1)}, u32[]{:S(2)}, u32[]{:S(2)}) collective-permute-start(bf16[2,16,4,2]{2,1,0,3:T(8,128)(2,1)S(1)} %get-tuple-element.121), channel_id=1, source_target_pairs={{0,64},{64,128},{128,192},{192,256},{256,320},{320,384},{384,448},... | collective-permute-start | bytes 1544 | tf_op jit(solution)/shard_map/ppermute | solution.py:22
  102.8 9.0 %collective-permute-start.15 = (bf16[2,16,4,2]{2,1,0,3:T(8,128)(2,1)S(1)}, bf16[2,16,4,2]{2,1,0,3:T(8,128)(2,1)S(1)}, u32[]{:S(2)}, u32[]{:S(2)}) collective-permute-start(bf16[2,16,4,2]{2,1,0,3:T(8,128)(2,1)S(1)} %get-tuple-element.122), channel_id=1, source_target_pairs={{64,0},{128,64},{192,128},{256,192},{320,256},{384,320},{448,384},... | collective-permute-start | bytes 1544 | tf_op jit(solution)/shard_map/ppermute | solution.py:23
  107.3 4.6 %collective-permute-start.8 = (bf16[2,4,8,256]{3,2,1,0:T(8,128)(2,1)S(1)}, bf16[2,4,8,256]{3,2,1,0:T(8,128)(2,1)S(1)}, u32[]{:S(2)}, u32[]{:S(2)}) collective-permute-start(bf16[2,4,8,256]{3,2,1,0:T(8,128)(2,1)S(1)} %get-tuple-element.119), channel_id=1, source_target_pairs={{0,1},{1,2},{2,3},{3,4},{4,5},{5,6},{6,7},{7,8},{8,9},{9,10},{10,1... | collective-permute-start | bytes 98312 | tf_op jit(solution)/shard_map/ppermute | solution.py:22
  109.8 9.5 %collective-permute-start.9 = (bf16[2,4,8,256]{3,2,1,0:T(8,128)(2,1)S(1)}, bf16[2,4,8,256]{3,2,1,0:T(8,128)(2,1)S(1)}, u32[]{:S(2)}, u32[]{:S(2)}) collective-permute-start(bf16[2,4,8,256]{3,2,1,0:T(8,128)(2,1)S(1)} %get-tuple-element.120), channel_id=1, source_target_pairs={{1,0},{2,1},{3,2},{4,3},{5,4},{6,5},{7,6},{8,7},{9,8},{10,9},{11,1... | collective-permute-start | bytes 98312 | tf_op jit(solution)/shard_map/ppermute | solution.py:23
  119.3 7.5 %collective-permute-start.10 = (bf16[2,16,4,256]{3,2,1,0:T(4,128)(2,1)S(1)}, bf16[2,16,4,256]{3,2,1,0:T(4,128)(2,1)S(1)}, u32[]{:S(2)}, u32[]{:S(2)}) collective-permute-start(bf16[2,16,4,256]{3,2,1,0:T(4,128)(2,1)S(1)} %get-tuple-element.117), channel_id=1, source_target_pairs={{0,64},{64,128},{128,192},{192,256},{256,320},{320,384},{384,448},... | collective-permute-start | bytes 196616 | tf_op jit(solution)/shard_map/ppermute | solution.py:22
  121.3 6.8 %collective-permute-start.11 = (bf16[2,16,4,256]{3,2,1,0:T(4,128)(2,1)S(1)}, bf16[2,16,4,256]{3,2,1,0:T(4,128)(2,1)S(1)}, u32[]{:S(2)}, u32[]{:S(2)}) collective-permute-start(bf16[2,16,4,256]{3,2,1,0:T(4,128)(2,1)S(1)} %get-tuple-element.118), channel_id=1, source_target_pairs={{64,0},{128,64},{192,128},{256,192},{320,256},{384,320},{448,384},... | collective-permute-start | bytes 196616 | tf_op jit(solution)/shard_map/ppermute | solution.py:23
  148.2 6.9 %collective-permute-start.16 = (f32[16,2,1,128]{0,3,2,1:T(8,128)S(1)}, f32[16,2,1,128]{0,3,2,1:T(8,128)S(1)}, u32[]{:S(2)}, u32[]{:S(2)}) collective-permute-start(f32[16,2,1,128]{0,3,2,1:T(8,128)S(1)} %get-tuple-element.43), channel_id=1, source_target_pairs={{0,1},{1,2},{2,3},{3,4},{4,5},{5,6},{6,7},{7,8},{8,9},{9,10},{10,1... | collective-permute-start | bytes 49160 | tf_op jit(solution)/shard_map/ppermute | solution.py:22
  153.0 12.0 %collective-permute-start.17 = (f32[16,2,1,128]{0,3,2,1:T(8,128)S(1)}, f32[16,2,1,128]{0,3,2,1:T(8,128)S(1)}, u32[]{:S(2)}, u32[]{:S(2)}) collective-permute-start(f32[16,2,1,128]{0,3,2,1:T(8,128)S(1)} %get-tuple-element.44), channel_id=1, source_target_pairs={{1,0},{2,1},{3,2},{4,3},{5,4},{6,5},{7,6},{8,7},{9,8},{10,9},{11,1... | collective-permute-start | bytes 49160 | tf_op jit(solution)/shard_map/ppermute | solution.py:23
  166.0 4.3 %collective-permute-start.18 = (f32[16,2,1,128]{0,3,2,1:T(8,128)S(1)}, f32[16,2,1,128]{0,3,2,1:T(8,128)S(1)}, u32[]{:S(2)}, u32[]{:S(2)}) collective-permute-start(f32[16,2,1,128]{0,3,2,1:T(8,128)S(1)} %get-tuple-element.41), channel_id=1, source_target_pairs={{0,1},{1,2},{2,3},{3,4},{4,5},{5,6},{6,7},{7,8},{8,9},{9,10},{10,1... | collective-permute-start | bytes 49160 | tf_op jit(solution)/shard_map/ppermute | solution.py:22
  167.9 11.2 %collective-permute-start.19 = (f32[16,2,1,128]{0,3,2,1:T(8,128)S(1)}, f32[16,2,1,128]{0,3,2,1:T(8,128)S(1)}, u32[]{:S(2)}, u32[]{:S(2)}) collective-permute-start(f32[16,2,1,128]{0,3,2,1:T(8,128)S(1)} %get-tuple-element.42), channel_id=1, source_target_pairs={{1,0},{2,1},{3,2},{4,3},{5,4},{6,5},{7,6},{8,7},{9,8},{10,9},{11,1... | collective-permute-start | bytes 49160 | tf_op jit(solution)/shard_map/ppermute | solution.py:23
  180.1 4.3 %collective-permute-start.20 = (f32[16,2,1,128]{0,3,2,1:T(8,128)S(1)}, f32[16,2,1,128]{0,3,2,1:T(8,128)S(1)}, u32[]{:S(2)}, u32[]{:S(2)}) collective-permute-start(f32[16,2,1,128]{0,3,2,1:T(8,128)S(1)} %get-tuple-element.39), channel_id=1, source_target_pairs={{0,1},{1,2},{2,3},{3,4},{4,5},{5,6},{6,7},{7,8},{8,9},{9,10},{10,1... | collective-permute-start | bytes 49160 | tf_op jit(solution)/shard_map/ppermute | solution.py:22
  182.0 10.6 %collective-permute-start.21 = (f32[16,2,1,128]{0,3,2,1:T(8,128)S(1)}, f32[16,2,1,128]{0,3,2,1:T(8,128)S(1)}, u32[]{:S(2)}, u32[]{:S(2)}) collective-permute-start(f32[16,2,1,128]{0,3,2,1:T(8,128)S(1)} %get-tuple-element.40), channel_id=1, source_target_pairs={{1,0},{2,1},{3,2},{4,3},{5,4},{6,5},{7,6},{8,7},{9,8},{10,9},{11,1... | collective-permute-start | bytes 49160 | tf_op jit(solution)/shard_map/ppermute | solution.py:23
  193.6 4.3 %collective-permute-start.22 = (f32[16,2,1,128]{0,3,2,1:T(8,128)S(1)}, f32[16,2,1,128]{0,3,2,1:T(8,128)S(1)}, u32[]{:S(2)}, u32[]{:S(2)}) collective-permute-start(f32[16,2,1,128]{0,3,2,1:T(8,128)S(1)} %get-tuple-element.37), channel_id=1, source_target_pairs={{0,1},{1,2},{2,3},{3,4},{4,5},{5,6},{6,7},{7,8},{8,9},{9,10},{10,1... | collective-permute-start | bytes 49160 | tf_op jit(solution)/shard_map/ppermute | solution.py:22
  195.5 10.5 %collective-permute-start.23 = (f32[16,2,1,128]{0,3,2,1:T(8,128)S(1)}, f32[16,2,1,128]{0,3,2,1:T(8,128)S(1)}, u32[]{:S(2)}, u32[]{:S(2)}) collective-permute-start(f32[16,2,1,128]{0,3,2,1:T(8,128)S(1)} %get-tuple-element.38), channel_id=1, source_target_pairs={{1,0},{2,1},{3,2},{4,3},{5,4},{6,5},{7,6},{8,7},{9,8},{10,9},{11,1... | collective-permute-start | bytes 49160 | tf_op jit(solution)/shard_map/ppermute | solution.py:23
where the time goes:
time: 209 us; the launch traced here: 208 us
  waiting for transfers between devices  94.1 us (45%)
  starting transfers between devices  80.5 us (39%)
  blocking collectives  13 us (6%)
  local copies, waits for them, and re-layouts  8.04 us (4%)
  other arithmetic  5.61 us (3%)
  matrix products  4.99 us (2%)
    ppermute x12, waiting for transfers between devices, with_halo(): after = lax.ppermute(initial, axis, down)  86.2 us
    ppermute x12, starting transfers between devices, with_halo(): after = lax.ppermute(initial, axis, down)  32.3 us
    ppermute x12, starting transfers between devices, with_halo(): before = lax.ppermute(last, axis, up)  31.7 us
    all_to_all x1, starting transfers between devices, local(): lax.all_to_all(sending, 'mem', split_axis=1, concat_axis=0, tiled=True)  16.5 us
    all_to_all x1, blocking collectives, local(): lax.all_to_all(returning, 'mem', split_axis=0, concat_axis=1, tiled=True)  13 us
    all_to_all x1, waiting for transfers between devices, local(): lax.all_to_all(sending, 'mem', split_axis=1, concat_axis=0, tiled=True)  7.84 us
  transfers between devices with their start and end apart: 25, of which 12 were waited for; matrix products, arithmetic and copies ran while one was open for 0% of the time, Pallas kernels for 0%

commit v1 on v0

v1 whole, which is shorter than its diff:
```python
import functools

import jax
import jax.numpy as jnp
from jax import lax
from jax.experimental import pallas as pl
from jax.experimental.pallas import tpu as pltpu
from jax.sharding import PartitionSpec as P

PATCH = 8
RADIUS = 4
FSTEPS = 4
CADV = 0.05
LANES = 128
MESH = pl.DeviceIdType.MESH
HIGHEST = lax.Precision.HIGHEST
BF16 = jnp.bfloat16
F32 = jnp.float32
I16 = jnp.int16
LIMIT = 32766.0
BOUND = 6.0


def lane_roll(value, shift):
    return pltpu.roll(value, shift % LANES, value.ndim - 1)


def advance(above, here, below):
    u_field, v_field = here

    def tendency(f):
        along_x = lane_roll(here[f], -1) - lane_roll(here[f], 1)
        along_y = below[f] - above[f]
        return here[f] - CADV * (u_field * along_x + v_field * along_y)

    return tendency(0), tendency(1)


def forecast_rows(rows):
    history = [[] for _ in range(FSTEPS)]
    done = []
    for row in rows:
        current = row
        for level in history:
            level.append(current)
            if len(level) < 3:
                current = None
                break
            current = advance(*level[-3:])
        if current is not None:
            done.append(current)
    return done


def swap_chunks(tiles):
    tiles = list(tiles)
    chunk = lax.broadcasted_iota(jnp.int32, tiles[0].shape, tiles[0].ndim - 1) // 8
    for bit in (1, 2, 4, 8):
        clear = (chunk & bit) == 0
        for i in range(16):
            if i & bit == 0:
                first, second = tiles[i], tiles[i | bit]
                tiles[i] = jnp.where(clear, first, lane_roll(second, 8 * bit))
                tiles[i | bit] = jnp.where(clear, lane_roll(first, -8 * bit), second)
    return tiles


def kernel(
    n_mem, n_rows,
    x_ref, values_ref, variance_ref, mask_ref, out_ref,
    band, band_above, band_below,
    obs, obs_above, obs_below, obs_wide, obs_left, obs_right,
    chunks, regions, unit, units, analysed, edges, own_part, above_part, below_part,
    band_send, band_recv, obs_send, obs_recv,
    region_send, region_recv, unit_send, unit_recv, own_send, own_recv, down_send, down_recv, up_send, up_recv,
):
    members = n_mem * 16
    me_mem, me_row = lax.axis_index("mem"), lax.axis_index("rows")
    above, below = lax.rem(me_row + n_rows - 1, n_rows), lax.rem(me_row + 1, n_rows)
    left, right = lax.rem(me_mem + n_mem - 1, n_mem), lax.rem(me_mem + 1, n_mem)

    def at(mem, row):
        return {"mem": mem, "rows": row}

    def remote(src, dst, send, recv, mem, row):
        return pltpu.make_async_remote_copy(
            src_ref=src, dst_ref=dst, send_sem=send, recv_sem=recv,
            device_id=at(mem, row), device_id_type=MESH,
        )

    offsets = sorted(range(1, n_mem), key=lambda d: -min(d, n_mem - d))
    partners = [lax.rem(me_mem + d, n_mem) for d in offsets]

    barrier = pltpu.get_barrier_semaphore()
    for row in (above, below):
        pl.semaphore_signal(barrier, inc=1, device_id=at(me_mem, row), device_id_type=MESH)
    for partner in partners:
        pl.semaphore_signal(barrier, inc=1, device_id=at(partner, me_row), device_id_type=MESH)

    own_rows = []
    for r in range(PATCH):
        row = tuple(lane_roll(x_ref[r, f], RADIUS) for f in range(2))
        own_rows.append(row)
        for f in range(2):
            band[r, f] = jnp.round(row[f] * (LIMIT / BOUND)).astype(I16)

    weight = (mask_ref[...].astype(F32) * variance_ref[...]).astype(BF16).astype(F32)
    planes = jnp.concatenate(
        [weight.reshape(2 * PATCH, PATCH), values_ref[...].reshape(2 * PATCH, PATCH)], 0
    )
    spread = (
        lax.broadcasted_iota(jnp.int32, (PATCH, LANES), 1) % 8
        == lax.broadcasted_iota(jnp.int32, (PATCH, LANES), 0)
    ).astype(F32)
    wide = jnp.dot(planes, spread, precision=HIGHEST, preferred_element_type=F32)
    wide = wide.reshape(4, PATCH, LANES)
    keep = (
        lax.broadcasted_iota(jnp.int32, wide.shape, 2) // 8
        == lax.broadcasted_iota(jnp.int32, wide.shape, 1) + RADIUS
    )
    wide = jnp.sum(jnp.where(keep, wide, 0.0), 1)
    obs[...] = jnp.concatenate([wide, jnp.zeros((4, LANES), F32)], 0)

    pl.semaphore_wait(barrier, n_mem + 1)

    to_below = remote(band, band_above, band_send.at[0], band_recv.at[0], me_mem, below)
    to_above = remote(band, band_below, band_send.at[1], band_recv.at[1], me_mem, above)
    to_below.start()
    to_above.start()
    obs_copies = [
        remote(obs, obs_above, obs_send.at[0], obs_recv.at[0], me_mem, below),
        remote(obs, obs_below, obs_send.at[1], obs_recv.at[1], me_mem, above),
        remote(obs_wide, obs_left, obs_send.at[2], obs_recv.at[2], right, me_row),
        remote(obs_wide, obs_right, obs_send.at[3], obs_recv.at[3], left, me_row),
    ]
    obs_copies[0].start()
    obs_copies[1].start()

    to_below.wait_recv()
    to_above.wait_recv()

    def decoded(part, r):
        return tuple(part[r, f].astype(F32) * (BOUND / LIMIT) for f in range(2))

    rows = [decoded(band_above, r) for r in range(PATCH)]
    rows += own_rows
    rows += [decoded(band_below, r) for r in range(PATCH)]
    ready = forecast_rows(rows)
    largest = jnp.abs(ready[0][0])
    for row in ready:
        for f in range(2):
            largest = jnp.maximum(largest, jnp.abs(row[f]))
    largest = jnp.max(jnp.max(largest, 0, keepdims=True), 1, keepdims=True)
    largest = jnp.maximum(largest, 1e-30)
    unit[...] = jnp.broadcast_to(largest * (1.0 / LIMIT), (1, LANES))
    grain = jnp.broadcast_to(LIMIT / largest, ready[0][0].shape)
    for f in range(2):
        tiles = swap_chunks([row[f] for row in ready])
        for j in range(n_mem):
            chunks[j, f] = jnp.round(tiles[j] * grain).astype(I16)
        chunks[n_mem, f] = chunks[0, f]

    region_copies = []
    for d, partner in zip(offsets, partners):
        copy = remote(
            chunks.at[pl.ds(partner, 2)], regions.at[me_mem],
            region_send.at[d], region_recv.at[d], partner, me_row,
        )
        copy.start()
        region_copies.append(copy)
        copy = remote(
            unit, units.at[me_mem], unit_send.at[d], unit_recv.at[d], partner, me_row
        )
        copy.start()
        region_copies.append(copy)
    regions[me_mem] = chunks[pl.ds(me_mem, 2)]
    units[me_mem] = unit[...]

    lane = lax.broadcasted_iota(jnp.int32, (8, LANES), 1)
    obs_copies[0].wait_recv()
    obs_copies[1].wait_recv()
    turned = lane_roll(jnp.where(lane >= 64, obs_above[...], obs_below[...]), 64)
    extended = jnp.where((lane >= 32) & (lane < 96), obs[...], turned)
    obs_wide[...] = extended
    obs_copies[2].start()
    obs_copies[3].start()
    obs_copies[2].wait_recv()
    obs_copies[3].wait_recv()
    lower = lane % 8 < 4
    halves = (
        jnp.where(lower, lane_roll(obs_left[...], -4), lane_roll(extended, 4)),
        jnp.where(lower, lane_roll(extended, -4), lane_roll(obs_right[...], 4)),
    )
    order = [(h, f) for h in range(2) for f in range(2)]
    weight_row = jnp.concatenate([halves[h][f : f + 1] for h, f in order], 1)
    value_row = jnp.concatenate([halves[h][2 + f : 3 + f] for h, f in order], 1)
    point = lax.broadcasted_iota(jnp.int32, (1, 4 * LANES), 1)
    region_row = point % LANES // 8
    region_col = point // (2 * LANES) * 8 + point % 8

    def distance(index):
        return jnp.maximum(jnp.maximum(RADIUS - index, index - (RADIUS + PATCH - 1)), 0)

    far = jnp.maximum(distance(region_row), distance(region_col)).astype(F32)
    factor = weight_row * (1.0 - far / (RADIUS + 1.0))

    for copy in region_copies:
        copy.wait_recv()

    every_unit = units[...]
    sample = jnp.concatenate(
        [
            (regions[:, h, f].astype(F32) * every_unit).reshape(members, LANES)
            for h, f in order
        ],
        1,
    )
    mean = jnp.sum(sample, 0, keepdims=True) / members
    deviation = (sample - mean).astype(BF16)
    innovation = (value_row - mean).astype(BF16)
    wide_deviation = deviation.astype(F32)
    weighted = (wide_deviation * factor).astype(BF16)
    stacked = jnp.concatenate(
        [deviation, jnp.broadcast_to(innovation, (16, 4 * LANES))], 0
    )
    product = lax.dot_general(
        stacked, weighted, (((1,), (1,)), ((), ())), preferred_element_type=F32
    )
    gram, projected = product[:members], product[members : members + 8]
    eye = (
        lax.broadcasted_iota(jnp.int32, (members, members), 0)
        == lax.broadcasted_iota(jnp.int32, (members, members), 1)
    ).astype(F32)
    system = (members - 1.0) * eye + gram
    square = jnp.sum(jnp.sum(system * system, 1, keepdims=True), 0, keepdims=True)
    scale = jnp.sqrt(square)

    def mul(a, b):
        return jnp.dot(a, b, precision=HIGHEST, preferred_element_type=F32)

    first_y = system / scale
    middle = 1.5 * eye - 0.5 * first_y
    iter_z = middle
    iter_y = mul(first_y, middle)
    middle = 1.5 * eye - 0.5 * mul(iter_z, iter_y)
    iter_y = mul(iter_y, middle)
    iter_z = mul(middle, iter_z)
    middle = 1.5 * eye - 0.5 * mul(iter_z, iter_y)
    iter_z = mul(middle, iter_z)
    root = iter_z / jnp.sqrt(scale)
    shift = mul(mul(projected, root), root)[0:1]
    transform = ((members - 1.0) ** 0.5 * root + shift).astype(BF16)

    inner_lane = lax.broadcasted_iota(jnp.int32, (1, LANES), 1)

    def interior(wide_value):
        fields = []
        for f in range(2):
            low = wide_value[:, f * LANES : (f + 1) * LANES]
            high = wide_value[:, (2 + f) * LANES : (3 + f) * LANES]
            fields.append(
                jnp.where(inner_lane % 8 < 4, lane_roll(low, -4), lane_roll(high, 4))
            )
        centre = (inner_lane >= 32) & (inner_lane < 96)
        return jnp.where(centre, fields[0], lane_roll(fields[1], 64))

    inner = interior(wide_deviation).astype(BF16)
    increment = jnp.dot(transform, inner, preferred_element_type=F32)
    inner_mean = interior(jnp.broadcast_to(mean, (8, 4 * LANES)))[0:1]
    analysis = (inner_mean + increment).reshape(n_mem, 16, LANES)
    analysed[...] = analysis
    edges[...] = analysis.astype(BF16)

    return_copies = []
    for d, partner in list(zip(offsets, partners)) + [(0, me_mem)]:
        pieces = [
            (edges, above_part, down_send, down_recv, below),
            (edges, below_part, up_send, up_recv, above),
        ]
        if d:
            pieces.append((analysed, own_part, own_send, own_recv, me_row))
        for source, part, send, recv, row in pieces:
            copy = remote(
                source.at[partner], part.at[me_mem], send.at[d], recv.at[d], partner, row
            )
            copy.start()
            return_copies.append(copy)
    own_part[me_mem] = analysed[me_mem]
    for copy in return_copies:
        copy.wait_recv()

    own_tiles = swap_chunks([own_part[j] for j in range(n_mem)])
    chunk = lax.broadcasted_iota(jnp.int32, (16, LANES), 1) // 8
    from_above = ((chunk >= 8) & (chunk < 12)) | (chunk < 4)
    edge_tiles = swap_chunks(
        [
            jnp.where(from_above, above_part[j].astype(F32), below_part[j].astype(F32))
            for j in range(n_mem)
        ]
    )
    rows = [(edge_tiles[8 + i], edge_tiles[i]) for i in range(4)]
    rows += [(own_tiles[4 + i], own_tiles[(12 + i) % 16]) for i in range(PATCH)]
    rows += [(edge_tiles[4 + i], edge_tiles[12 + i]) for i in range(4)]
    for r, row in enumerate(forecast_rows(rows)):
        for f in range(2):
            out_ref[r, f] = row[f]

    to_below.wait_send()
    to_above.wait_send()
    for copy in obs_copies + region_copies + return_copies:
        copy.wait_send()


def local(sample_collection, obs_values, obs_inverse_variance, obs_mask):
    n_mem, n_rows = lax.axis_size("mem"), lax.axis_size("rows")
    local_members = sample_collection.shape[0]
    vmem = pl.BlockSpec(memory_space=pltpu.VMEM)
    dma = pltpu.SemaphoreType.DMA
    band = (PATCH, 2, local_members, LANES)
    part = (n_mem, local_members, LANES)
    result = pl.pallas_call(
        functools.partial(kernel, n_mem, n_rows),
        out_shape=jax.ShapeDtypeStruct(band, F32),
        in_specs=[vmem] * 4,
        out_specs=vmem,
        scratch_shapes=[
            pltpu.VMEM(band, I16),
            pltpu.VMEM(band, I16),
            pltpu.VMEM(band, I16),
        ]
        + [pltpu.VMEM((8, LANES), F32)] * 6
        + [
            pltpu.VMEM((n_mem + 1, 2, local_members, LANES), I16),
            pltpu.VMEM((n_mem, 2, 2, local_members, LANES), I16),
            pltpu.VMEM((1, LANES), F32),
            pltpu.VMEM((n_mem, 1, LANES), F32),
            pltpu.VMEM(part, F32),
            pltpu.VMEM(part, BF16),
            pltpu.VMEM(part, F32),
            pltpu.VMEM(part, BF16),
            pltpu.VMEM(part, BF16),
        ]
        + [dma((2,)), dma((2,)), dma((4,)), dma((4,))]
        + [dma((n_mem,))] * 10,
        compiler_params=pltpu.CompilerParams(collective_id=0, has_side_effects=True),
    )(
        jnp.transpose(sample_collection, (2, 1, 0, 3)),
        obs_values,
        obs_inverse_variance,
        obs_mask,
    )
    return jnp.transpose(result, (2, 1, 0, 3))


def solution(mesh):
    return jax.shard_map(
        local,
        mesh=mesh,
        in_specs=(
            P("mem", None, "rows", None),
            P(None, "rows", "mem"),
            P(None, "rows", "mem"),
            P(None, "rows", "mem"),
        ),
        out_specs=P("mem", None, "rows", None),
        check_vma=False,
    )
```

time: 209 us -> 52.9 us (0.25)
  the two profiles are of different devices: /device:TPU:61 before, /device:TPU:2 now
where the time goes in v1:
time: 52.9 us; the launch traced here: 52.7 us
  Pallas kernels  49.5 us (94%)
  local copies, waits for them, and re-layouts  3.24 us (6%)
    pallas_call x1, Pallas kernels, local(): pl.pallas_call(functools.partial(kernel, n_mem, n_rows), out_shape=jax.Sh...  49.5 us
    transpose x1, local copies, waits for them, and re-layouts, local(): return jnp.transpose(result, (2, 1, 0, 3))  1.64 us
    unnamed x1, local copies, waits for them, and re-layouts  1.6 us

profile of v1, /device:TPU:2, one launch (start us, length us, event | category | flops | bytes accessed | tf_op | source)
XLA Modules:
  0.0 52.7 jit_solution(906939825618572970)
XLA Ops:
  0.0 1.6 %copy.8 = f32[16,2,8,128]{3,0,1,2:T(8,128)} copy(f32[16,2,8,128]{3,2,1,0:T(8,128)} %param.4) | data formatting | bytes 262144 | tf_op args[0]
  1.6 49.5 %shard_map.46 = f32[8,2,16,128]{3,2,1,0:T(8,128)} custom-call(f32[8,2,16,128]{3,2,1,0:T(8,128)} %bitcast.5, f32[2,8,8]{2,1,0:T(8,128)} %values_ref.1, f32[2,8,8]{2,1,0:T(8,128)} %variance_ref.1, s32[2,8,8]{2,1,0:T(8,128)} %mask_ref.1), custom_call_target="tpu_custom_call" | custom-call | tf_op jit(solution)/shard_map/pallas_call | solution.py:321
  51.1 1.6 %copy.6 = f32[16,2,8,128]{3,2,1,0:T(8,128)} copy(f32[16,2,8,128]{3,0,1,2:T(8,128)} %bitcast.4) | data formatting | bytes 262144 | tf_op jit(solution)/shard_map/transpose | solution.py:352

commit v2 on v1

--- a/solution.py
+++ b/solution.py
@@ -68,10 +68,11 @@
 def kernel(
     n_mem, n_rows,
     x_ref, values_ref, variance_ref, mask_ref, out_ref,
+    x_local, values, variance, mask,
     band, band_above, band_below,
     obs, obs_above, obs_below, obs_wide, obs_left, obs_right,
     chunks, regions, unit, units, analysed, edges, own_part, above_part, below_part,
-    band_send, band_recv, obs_send, obs_recv,
+    rows_ready, mem_ready, load_sem, band_send, band_recv, obs_send, obs_recv,
     region_send, region_recv, unit_send, unit_recv, own_send, own_recv, down_send, down_recv, up_send, up_recv,
 ):
     members = n_mem * 16
@@ -92,21 +93,69 @@
     partners = [lax.rem(me_mem + d, n_mem) for d in offsets]
 
     barrier = pltpu.get_barrier_semaphore()
-    for row in (above, below):
-        pl.semaphore_signal(barrier, inc=1, device_id=at(me_mem, row), device_id_type=MESH)
+    even = lax.rem(me_row, 2) == 0
+    above_two = lax.rem(me_row + n_rows - 2, n_rows)
+    odd_row = me_row + 1 - lax.rem(me_row, 2)
+
+    def greet(semaphore, mem, row):
+        pl.semaphore_signal(semaphore, inc=1, device_id=at(mem, row), device_id_type=MESH)
+
+    @pl.when(even)
+    def _():
+        greet(barrier, me_mem, above_two)
+
+    @pl.when(jnp.logical_not(even))
+    def _():
+        greet(barrier, me_mem, below)
+        greet(barrier, me_mem, above)
+
     for partner in partners:
-        pl.semaphore_signal(barrier, inc=1, device_id=at(partner, me_row), device_id_type=MESH)
+        greet(barrier, partner, odd_row)
+
+    loads = [
+        pltpu.make_async_copy(source, target, load_sem.at[i])
+        for i, (source, target) in enumerate(
+            [
+                (x_ref, x_local),
+                (values_ref, values),
+                (variance_ref, variance),
+                (mask_ref, mask),
+            ]
+        )
+    ]
+    for load in loads:
+        load.start()
+    loads[0].wait()
+
+    def rows_of(ref, r, f):
+        return ref.at[pl.ds(f * PATCH + r, 16, stride=2 * PATCH), :]
 
     own_rows = []
     for r in range(PATCH):
-        row = tuple(lane_roll(x_ref[r, f], RADIUS) for f in range(2))
+        row = tuple(lane_roll(rows_of(x_local, r, f)[...], RADIUS) for f in range(2))
         own_rows.append(row)
         for f in range(2):
             band[r, f] = jnp.round(row[f] * (LIMIT / BOUND)).astype(I16)
 
-    weight = (mask_ref[...].astype(F32) * variance_ref[...]).astype(BF16).astype(F32)
+    @pl.when(even)
+    def _():
+        pl.semaphore_wait(barrier, 3)
+        greet(rows_ready, me_mem, below)
+
+    @pl.when(jnp.logical_not(even))
+    def _():
+        pl.semaphore_wait(rows_ready, 1)
+
+    to_below = remote(band, band_above, band_send.at[0], band_recv.at[0], me_mem, below)
+    to_above = remote(band, band_below, band_send.at[1], band_recv.at[1], me_mem, above)
+    to_below.start()
+    to_above.start()
+
+    for load in loads[1:]:
+        load.wait()
+    weight = (mask[...].astype(F32) * variance[...]).astype(BF16).astype(F32)
     planes = jnp.concatenate(
-        [weight.reshape(2 * PATCH, PATCH), values_ref[...].reshape(2 * PATCH, PATCH)], 0
+        [weight.reshape(2 * PATCH, PATCH), values[...].reshape(2 * PATCH, PATCH)], 0
     )
     spread = (
         lax.broadcasted_iota(jnp.int32, (PATCH, LANES), 1) % 8
@@ -121,12 +170,6 @@
     wide = jnp.sum(jnp.where(keep, wide, 0.0), 1)
     obs[...] = jnp.concatenate([wide, jnp.zeros((4, LANES), F32)], 0)
 
-    pl.semaphore_wait(barrier, n_mem + 1)
-
-    to_below = remote(band, band_above, band_send.at[0], band_recv.at[0], me_mem, below)
-    to_above = remote(band, band_below, band_send.at[1], band_recv.at[1], me_mem, above)
-    to_below.start()
-    to_above.start()
     obs_copies = [
         remote(obs, obs_above, obs_send.at[0], obs_recv.at[0], me_mem, below),
         remote(obs, obs_below, obs_send.at[1], obs_recv.at[1], me_mem, above),
@@ -160,6 +203,15 @@
             chunks[j, f] = jnp.round(tiles[j] * grain).astype(I16)
         chunks[n_mem, f] = chunks[0, f]
 
+    @pl.when(jnp.logical_not(even))
+    def _():
+        pl.semaphore_wait(barrier, 2 * (n_mem - 1))
+        greet(mem_ready, me_mem, above)
+
+    @pl.when(even)
+    def _():
+        pl.semaphore_wait(mem_ready, 1)
+
     region_copies = []
     for d, partner in zip(offsets, partners):
         copy = remote(
@@ -236,7 +288,7 @@
     scale = jnp.sqrt(square)
 
     def mul(a, b):
-        return jnp.dot(a, b, precision=HIGHEST, preferred_element_type=F32)
+        return jnp.dot(a, b, precision=lax.Precision.HIGH, preferred_element_type=F32)
 
     first_y = system / scale
     middle = 1.5 * eye - 0.5 * first_y
@@ -303,7 +355,7 @@
     rows += [(edge_tiles[4 + i], edge_tiles[12 + i]) for i in range(4)]
     for r, row in enumerate(forecast_rows(rows)):
         for f in range(2):
-            out_ref[r, f] = row[f]
+            rows_of(out_ref, r, f)[...] = row[f]
 
     to_below.wait_send()
     to_above.wait_send()
@@ -314,16 +366,20 @@
 def local(sample_collection, obs_values, obs_inverse_variance, obs_mask):
     n_mem, n_rows = lax.axis_size("mem"), lax.axis_size("rows")
     local_members = sample_collection.shape[0]
-    vmem = pl.BlockSpec(memory_space=pltpu.VMEM)
     dma = pltpu.SemaphoreType.DMA
     band = (PATCH, 2, local_members, LANES)
+    flat = (local_members * 2 * PATCH, LANES)
     part = (n_mem, local_members, LANES)
     result = pl.pallas_call(
         functools.partial(kernel, n_mem, n_rows),
-        out_shape=jax.ShapeDtypeStruct(band, F32),
-        in_specs=[vmem] * 4,
-        out_specs=vmem,
+        out_shape=pltpu.VMEM(flat, F32),
+        in_specs=[pl.BlockSpec(memory_space=pl.ANY)] * 4,
+        out_specs=pl.BlockSpec(memory_space=pltpu.VMEM),
         scratch_shapes=[
+            pltpu.VMEM(flat, F32),
+            pltpu.VMEM(obs_values.shape, F32),
+            pltpu.VMEM(obs_values.shape, F32),
+            pltpu.VMEM(obs_values.shape, jnp.int32),
             pltpu.VMEM(band, I16),
             pltpu.VMEM(band, I16),
             pltpu.VMEM(band, I16),
@@ -340,16 +396,17 @@
             pltpu.VMEM(part, BF16),
             pltpu.VMEM(part, BF16),
         ]
-        + [dma((2,)), dma((2,)), dma((4,)), dma((4,))]
+        + [pltpu.SemaphoreType.REGULAR, pltpu.SemaphoreType.REGULAR]
+        + [dma((4,)), dma((2,)), dma((2,)), dma((4,)), dma((4,))]
         + [dma((n_mem,))] * 10,
         compiler_params=pltpu.CompilerParams(collective_id=0, has_side_effects=True),
     )(
-        jnp.transpose(sample_collection, (2, 1, 0, 3)),
+        sample_collection.reshape(flat),
         obs_values,
         obs_inverse_variance,
         obs_mask,
     )
-    return jnp.transpose(result, (2, 1, 0, 3))
+    return result.reshape(sample_collection.shape)
 
 
 def solution(mesh):

time: 52.9 us -> 48.8 us (0.922)
  local copies, waits for them, and re-layouts: 3.24 us -> 0.66 us
  Pallas kernels: 49.5 us -> 48 us
    transpose x1 -> x0, local copies, waits for them, and re-layouts: 1.64 us -> none  [local(): return jnp.transpose(result, (2, 1, 0, 3))]
    pallas_call x1, Pallas kernels: 49.5 us -> 48 us  [local(): pl.pallas_call(functools.partial(kernel, n_mem, n_rows), out_shape=pltpu....]
    unnamed x1, local copies, waits for them, and re-layouts: 1.6 us -> 0.66 us
where the time goes in v2:
time: 48.8 us; the launch traced here: 48.7 us
  Pallas kernels  48 us (98%)
  local copies, waits for them, and re-layouts  0.66 us (1%)
    pallas_call x1, Pallas kernels, local(): pl.pallas_call(functools.partial(kernel, n_mem, n_rows), out_shape=pltpu....  48 us

profile of v2, /device:TPU:2, one launch (start us, length us, event | category | flops | bytes accessed | tf_op | source)
XLA Modules:
  0.0 48.7 jit_solution(12244763302701710395)
XLA Ops:
  0.0 48.0 %shard_map.46 = f32[256,128]{1,0:T(8,128)S(1)} custom-call(f32[256,128]{1,0:T(8,128)} %bitcast.3, f32[2,8,8]{2,1,0:T(8,128)} %values_ref.1, f32[2,8,8]{2,1,0:T(8,128)} %variance_ref.1, s32[2,8,8]{2,1,0:T(8,128)} %mask_ref.1), custom_call_target="tpu_custom_call" | custom-call | tf_op jit(solution)/shard_map/pallas_call | solution.py:373
  48.0 0.7 %copy.6 = f32[16,2,8,128]{3,2,1,0:T(8,128)} copy(f32[16,2,8,128]{3,2,1,0:T(8,128)S(1)} %bitcast.2) | data formatting | bytes 262144

commit v3 on v2

--- a/solution.py
+++ b/solution.py
@@ -10,13 +10,13 @@
 PATCH = 8
 RADIUS = 4
 FSTEPS = 4
+SCHULZ_STEPS = 3
 CADV = 0.05
 LANES = 128
 MESH = pl.DeviceIdType.MESH
 HIGHEST = lax.Precision.HIGHEST
 BF16 = jnp.bfloat16
 F32 = jnp.float32
-I16 = jnp.int16
 LIMIT = 32766.0
 BOUND = 6.0
 
@@ -65,15 +65,36 @@
     return tiles
 
 
+def top_lanes(shape):
+    chunk = lax.broadcasted_iota(jnp.int32, shape, len(shape) - 1) // 8
+    return (chunk & 4) != 0
+
+
+def pair_codes(low, high):
+    low, high = (jnp.round(v).astype(jnp.int32) for v in (low, high))
+    return (high << 16) | (low & 0xFFFF)
+
+
+def codes_of(word):
+    return ((word << 16) >> 16).astype(F32), (word >> 16).astype(F32)
+
+
+def unit_of(values):
+    largest = functools.reduce(jnp.maximum, [jnp.abs(v) for v in values])
+    largest = jnp.max(jnp.max(largest, 0, keepdims=True), 1, keepdims=True)
+    largest = jnp.maximum(largest, 1e-30)
+    return jnp.broadcast_to(largest * (1.0 / LIMIT), (1, LANES)), LIMIT / largest
+
+
 def kernel(
     n_mem, n_rows,
     x_ref, values_ref, variance_ref, mask_ref, out_ref,
     x_local, values, variance, mask,
     band, band_above, band_below,
     obs, obs_above, obs_below, obs_wide, obs_left, obs_right,
-    chunks, regions, unit, units, analysed, edges, own_part, above_part, below_part,
-    rows_ready, mem_ready, load_sem, band_send, band_recv, obs_send, obs_recv,
-    region_send, region_recv, unit_send, unit_recv, own_send, own_recv, down_send, down_recv, up_send, up_recv,
+    chunks, regions, unit, units, back_unit, back_units, analysed, edges_up, edges_down, own_part, above_part, below_part,
+    token, load_sem, band_send, band_recv, obs_send, obs_recv,
+    region_send, region_recv, unit_send, unit_recv, own_send, own_recv, back_send, back_recv, down_send, down_recv, up_send, up_recv,
 ):
     members = n_mem * 16
     me_mem, me_row = lax.axis_index("mem"), lax.axis_index("rows")
@@ -93,24 +114,19 @@
     partners = [lax.rem(me_mem + d, n_mem) for d in offsets]
 
     barrier = pltpu.get_barrier_semaphore()
-    even = lax.rem(me_row, 2) == 0
-    above_two = lax.rem(me_row + n_rows - 2, n_rows)
-    odd_row = me_row + 1 - lax.rem(me_row, 2)
+
+    def ring(mem, step):
+        return lax.rem(mem + step + n_mem, n_mem)
 
     def greet(semaphore, mem, row):
         pl.semaphore_signal(semaphore, inc=1, device_id=at(mem, row), device_id_type=MESH)
 
-    @pl.when(even)
-    def _():
-        greet(barrier, me_mem, above_two)
-
-    @pl.when(jnp.logical_not(even))
-    def _():
-        greet(barrier, me_mem, below)
-        greet(barrier, me_mem, above)
-
-    for partner in partners:
-        greet(barrier, partner, odd_row)
+    pair = me_mem + 1 - 2 * lax.rem(me_mem, 2)
+    near = [pair] + [ring(mem, step) for mem in (me_mem, pair) for step in (4, -4, 2, -2)]
+    for row in (above, below):
+        greet(barrier, me_mem, row)
+    for mem in near:
+        greet(barrier, mem, me_row)
 
     loads = [
         pltpu.make_async_copy(source, target, load_sem.at[i])
@@ -134,22 +150,16 @@
     for r in range(PATCH):
         row = tuple(lane_roll(rows_of(x_local, r, f)[...], RADIUS) for f in range(2))
         own_rows.append(row)
-        for f in range(2):
-            band[r, f] = jnp.round(row[f] * (LIMIT / BOUND)).astype(I16)
-
-    @pl.when(even)
-    def _():
-        pl.semaphore_wait(barrier, 3)
-        greet(rows_ready, me_mem, below)
-
-    @pl.when(jnp.logical_not(even))
-    def _():
-        pl.semaphore_wait(rows_ready, 1)
+        band[r] = pair_codes(*(value * (LIMIT / BOUND) for value in row))
+
+    pl.semaphore_wait(barrier, 2 + len(near))
 
     to_below = remote(band, band_above, band_send.at[0], band_recv.at[0], me_mem, below)
     to_above = remote(band, band_below, band_send.at[1], band_recv.at[1], me_mem, above)
     to_below.start()
     to_above.start()
+    for step in (4, -4):
+        greet(token, ring(me_mem, step), me_row)
 
     for load in loads[1:]:
         load.wait()
@@ -182,50 +192,34 @@
     to_below.wait_recv()
     to_above.wait_recv()
 
-    def decoded(part, r):
-        return tuple(part[r, f].astype(F32) * (BOUND / LIMIT) for f in range(2))
-
-    rows = [decoded(band_above, r) for r in range(PATCH)]
-    rows += own_rows
-    rows += [decoded(band_below, r) for r in range(PATCH)]
-    ready = forecast_rows(rows)
-    largest = jnp.abs(ready[0][0])
-    for row in ready:
-        for f in range(2):
-            largest = jnp.maximum(largest, jnp.abs(row[f]))
-    largest = jnp.max(jnp.max(largest, 0, keepdims=True), 1, keepdims=True)
-    largest = jnp.maximum(largest, 1e-30)
-    unit[...] = jnp.broadcast_to(largest * (1.0 / LIMIT), (1, LANES))
-    grain = jnp.broadcast_to(LIMIT / largest, ready[0][0].shape)
-    for f in range(2):
-        tiles = swap_chunks([row[f] for row in ready])
+    def rows_in(part, half):
+        words = [part[r, 8 * half : 8 * half + 8] for r in range(PATCH)]
+        return [tuple(v * (BOUND / LIMIT) for v in codes_of(word)) for word in words]
+
+    for half in range(2):
+        rows = rows_in(band_above, half)
+        rows += [tuple(v[8 * half : 8 * half + 8] for v in row) for row in own_rows]
+        rows += rows_in(band_below, half)
+        ready = forecast_rows(rows)
+        unit[half], grain = unit_of([v for row in ready for v in row])
+        grain = jnp.broadcast_to(grain, (8, LANES))
+        tiles = swap_chunks([pair_codes(*(v * grain for v in row)) for row in ready])
         for j in range(n_mem):
-            chunks[j, f] = jnp.round(tiles[j] * grain).astype(I16)
-        chunks[n_mem, f] = chunks[0, f]
-
-    @pl.when(jnp.logical_not(even))
-    def _():
-        pl.semaphore_wait(barrier, 2 * (n_mem - 1))
-        greet(mem_ready, me_mem, above)
-
-    @pl.when(even)
-    def _():
-        pl.semaphore_wait(mem_ready, 1)
-
-    region_copies = []
-    for d, partner in zip(offsets, partners):
-        copy = remote(
-            chunks.at[pl.ds(partner, 2)], regions.at[me_mem],
-            region_send.at[d], region_recv.at[d], partner, me_row,
-        )
-        copy.start()
-        region_copies.append(copy)
-        copy = remote(
-            unit, units.at[me_mem], unit_send.at[d], unit_recv.at[d], partner, me_row
-        )
-        copy.start()
-        region_copies.append(copy)
-    regions[me_mem] = chunks[pl.ds(me_mem, 2)]
+            chunks[half, j] = tiles[j]
+        chunks[half, n_mem] = tiles[0]
+
+        if half == 0:
+            pl.semaphore_wait(token, 2)
+
+        for partner in partners:
+            remote(
+                chunks.at[half, pl.ds(partner, 2)], regions.at[me_mem, half],
+                region_send, region_recv, partner, me_row,
+            ).start()
+    for partner in partners:
+        remote(unit, units.at[me_mem], unit_send, unit_recv, partner, me_row).start()
+    for half in range(2):
+        regions[me_mem, half] = chunks[half, pl.ds(me_mem, 2)]
     units[me_mem] = unit[...]
 
     lane = lax.broadcasted_iota(jnp.int32, (8, LANES), 1)
@@ -256,22 +250,38 @@
     far = jnp.maximum(distance(region_row), distance(region_col)).astype(F32)
     factor = weight_row * (1.0 - far / (RADIUS + 1.0))
 
-    for copy in region_copies:
-        copy.wait_recv()
+    column = lax.broadcasted_iota(jnp.int32, (4 * LANES, 2 * LANES), 1)
+    lane = column % LANES
+    turn = jnp.where((lane & 32) != 0, 32, LANES - 32)
+    lane = jnp.where(column < LANES, lane, (lane + turn) % LANES)
+    field = 1 - ((lane >= 32) & (lane < 96)).astype(jnp.int32)
+    grid_row = (lane // 8 + 8 * field) % 16
+    grid_col = lane % 8 + RADIUS
+    source = (grid_col // 8 * 2 + field) * LANES + grid_row * 8 + grid_col % 8
+    select = (lax.broadcasted_iota(jnp.int32, lane.shape, 0) == source).astype(BF16)
+
+    others = n_mem - 1
+
+    def whole(buffer, count, send, recv):
+        part = buffer.at[pl.ds(0, count)]
+        return remote(part, part, send, recv, right, me_row)
+
+    region_all = whole(regions, others, region_send, region_recv)
+    unit_all = whole(units, others, unit_send, unit_recv)
+    region_all.wait_recv()
+    unit_all.wait_recv()
 
     every_unit = units[...]
-    sample = jnp.concatenate(
-        [
-            (regions[:, h, f].astype(F32) * every_unit).reshape(members, LANES)
-            for h, f in order
-        ],
-        1,
-    )
+    fields = []
+    for h in range(2):
+        for code in codes_of(regions[:, :, h]):
+            fields.append((code * every_unit).reshape(members, LANES))
+    sample = jnp.concatenate(fields, 1)
     mean = jnp.sum(sample, 0, keepdims=True) / members
     deviation = (sample - mean).astype(BF16)
     innovation = (value_row - mean).astype(BF16)
-    wide_deviation = deviation.astype(F32)
-    weighted = (wide_deviation * factor).astype(BF16)
+    weighted = (deviation.astype(F32) * factor).astype(BF16)
+    inner = jnp.dot(deviation, select, preferred_element_type=F32).astype(BF16)
     stacked = jnp.concatenate(
         [deviation, jnp.broadcast_to(innovation, (16, 4 * LANES))], 0
     )
@@ -288,19 +298,26 @@
     scale = jnp.sqrt(square)
 
     def mul(a, b):
-        return jnp.dot(a, b, precision=lax.Precision.HIGH, preferred_element_type=F32)
-
-    first_y = system / scale
-    middle = 1.5 * eye - 0.5 * first_y
-    iter_z = middle
-    iter_y = mul(first_y, middle)
-    middle = 1.5 * eye - 0.5 * mul(iter_z, iter_y)
-    iter_y = mul(iter_y, middle)
-    iter_z = mul(middle, iter_z)
-    middle = 1.5 * eye - 0.5 * mul(iter_z, iter_y)
-    iter_z = mul(middle, iter_z)
-    root = iter_z / jnp.sqrt(scale)
-    shift = mul(mul(projected, root), root)[0:1]
+        return jnp.dot(a.astype(BF16), b.astype(BF16), preferred_element_type=F32)
+
+    y = system * (1.0 / scale)
+    y2 = mul(y, y)
+    y3 = mul(y, y2)
+    y4 = mul(y2, y2)
+    y5 = mul(y2, y3)
+    zy1 = 2.25 * y - 1.5 * y2 + 0.25 * y3
+    zyy1 = 2.25 * y2 - 1.5 * y3 + 0.25 * y4
+    zyyy1 = 2.25 * y3 - 1.5 * y4 + 0.25 * y5
+    e2 = 0.25 * zyy1 - 0.75 * (y + zy1)
+    iter_y = 2.25 * y - 0.75 * (y2 + zyy1) + 0.25 * zyyy1
+    zy2 = 2.25 * iter_y + mul(e2, iter_y)
+    e3 = 1.5 * e2 - 1.125 * zy2 - 0.5 * mul(zy2, e2)
+    lead = (1.5**SCHULZ_STEPS) * eye
+    shrink = lax.rsqrt(scale)
+    root = (lead + e3) * shrink
+    half_way = (1.5**SCHULZ_STEPS) * projected + mul(projected, e3)
+    shift = ((1.5**SCHULZ_STEPS) * half_way + mul(half_way, e3)) / scale
+    shift = shift[0:1]
     transform = ((members - 1.0) ** 0.5 * root + shift).astype(BF16)
 
     inner_lane = lax.broadcasted_iota(jnp.int32, (1, LANES), 1)
@@ -316,60 +333,93 @@
         centre = (inner_lane >= 32) & (inner_lane < 96)
         return jnp.where(centre, fields[0], lane_roll(fields[1], 64))
 
-    inner = interior(wide_deviation).astype(BF16)
     increment = jnp.dot(transform, inner, preferred_element_type=F32)
     inner_mean = interior(jnp.broadcast_to(mean, (8, 4 * LANES)))[0:1]
-    analysis = (inner_mean + increment).reshape(n_mem, 16, LANES)
-    analysed[...] = analysis
-    edges[...] = analysis.astype(BF16)
-
-    return_copies = []
-    for d, partner in list(zip(offsets, partners)) + [(0, me_mem)]:
-        pieces = [
-            (edges, above_part, down_send, down_recv, below),
-            (edges, below_part, up_send, up_recv, above),
-        ]
-        if d:
-            pieces.append((analysed, own_part, own_send, own_recv, me_row))
-        for source, part, send, recv, row in pieces:
-            copy = remote(
-                source.at[partner], part.at[me_mem], send.at[d], recv.at[d], partner, row
-            )
-            copy.start()
-            return_copies.append(copy)
+    top = top_lanes((8, LANES))
+    mean_rows = jnp.broadcast_to(inner_mean, (8, LANES))
+    turned_mean = jnp.where(top, lane_roll(mean_rows, -32), lane_roll(mean_rows, 32))[0:1]
+    analysis = inner_mean + increment[:, :LANES]
+    turned = turned_mean + increment[:, LANES:]
+    parts = (n_mem, 2, 8, LANES)
+    first, second = analysis.reshape(parts)[:, 0], turned.reshape(parts)[:, 1]
+    top = top_lanes(first.shape)
+    edges_up[...] = jnp.where(top, first, second).astype(BF16)
+    edges_down[...] = jnp.where(top, second, first).astype(BF16)
+
+    for partner in partners + [me_mem]:
+        remote(
+            edges_down.at[partner], above_part.at[me_mem], down_send, down_recv, partner, below
+        ).start()
+        remote(
+            edges_up.at[partner], below_part.at[me_mem], up_send, up_recv, partner, above
+        ).start()
+    back_unit[...], grain = unit_of([analysis])
+    scaled = (analysis * grain).reshape(parts)
+    analysed[...] = pair_codes(scaled[:, 0], scaled[:, 1])
+    for partner in partners:
+        remote(
+            analysed.at[partner], own_part.at[me_mem], own_send, own_recv, partner, me_row
+        ).start()
+    for partner in partners:
+        remote(
+            back_unit, back_units.at[me_mem], back_send, back_recv, partner, me_row
+        ).start()
     own_part[me_mem] = analysed[me_mem]
-    for copy in return_copies:
-        copy.wait_recv()
-
-    own_tiles = swap_chunks([own_part[j] for j in range(n_mem)])
-    chunk = lax.broadcasted_iota(jnp.int32, (16, LANES), 1) // 8
-    from_above = ((chunk >= 8) & (chunk < 12)) | (chunk < 4)
+    back_units[me_mem] = back_unit[...]
+    to_below.wait_send()
+    to_above.wait_send()
+    for copy in obs_copies:
+        copy.wait_send()
+    region_all.wait_send()
+    unit_all.wait_send()
+    down_all = whole(above_part, n_mem, down_send, down_recv)
+    up_all = whole(below_part, n_mem, up_send, up_recv)
+    own_all = whole(own_part, others, own_send, own_recv)
+    back_all = whole(back_units, others, back_send, back_recv)
+    own_all.wait_recv()
+    back_all.wait_recv()
+    source = lax.broadcasted_iota(jnp.int32, (n_mem, LANES), 0)
+    lane = lax.broadcasted_iota(jnp.int32, (n_mem, LANES), 1)
+    unit_row = jnp.sum(
+        jnp.where(lane // 8 == source, back_units[...].reshape(n_mem, LANES), 0.0),
+        0,
+        keepdims=True,
+    )
+    own_tiles = [
+        jnp.concatenate([v * unit_row for v in codes_of(tile)], 0)
+        for tile in swap_chunks([own_part[j] for j in range(n_mem)])
+    ]
+    down_all.wait_recv()
+    up_all.wait_recv()
     edge_tiles = swap_chunks(
         [
-            jnp.where(from_above, above_part[j].astype(F32), below_part[j].astype(F32))
+            jnp.concatenate([below_part[j].astype(F32), above_part[j].astype(F32)], 0)
             for j in range(n_mem)
         ]
     )
-    rows = [(edge_tiles[8 + i], edge_tiles[i]) for i in range(4)]
+
+    def edge_row(part, first, second):
+        pick = slice(8 * part, 8 * part + 8)
+        return jnp.concatenate([edge_tiles[first][pick], edge_tiles[second][pick]], 0)
+
+    rows = [(edge_row(1, 8 + i, 4 + i), edge_row(1, i, 12 + i)) for i in range(4)]
     rows += [(own_tiles[4 + i], own_tiles[(12 + i) % 16]) for i in range(PATCH)]
-    rows += [(edge_tiles[4 + i], edge_tiles[12 + i]) for i in range(4)]
+    rows += [(edge_row(0, 4 + i, 8 + i), edge_row(0, 12 + i, i)) for i in range(4)]
     for r, row in enumerate(forecast_rows(rows)):
         for f in range(2):
             rows_of(out_ref, r, f)[...] = row[f]
 
-    to_below.wait_send()
-    to_above.wait_send()
-    for copy in obs_copies + region_copies + return_copies:
-        copy.wait_send()
+    for copies in (own_all, back_all, down_all, up_all):
+        copies.wait_send()
 
 
 def local(sample_collection, obs_values, obs_inverse_variance, obs_mask):
     n_mem, n_rows = lax.axis_size("mem"), lax.axis_size("rows")
     local_members = sample_collection.shape[0]
     dma = pltpu.SemaphoreType.DMA
-    band = (PATCH, 2, local_members, LANES)
+    band = (PATCH, local_members, LANES)
     flat = (local_members * 2 * PATCH, LANES)
-    part = (n_mem, local_members, LANES)
+    part = (n_mem, local_members // 2, LANES)
     result = pl.pallas_call(
         functools.partial(kernel, n_mem, n_rows),
         out_shape=pltpu.VMEM(flat, F32),
@@ -380,25 +430,26 @@
             pltpu.VMEM(obs_values.shape, F32),
             pltpu.VMEM(obs_values.shape, F32),
             pltpu.VMEM(obs_values.shape, jnp.int32),
-            pltpu.VMEM(band, I16),
-            pltpu.VMEM(band, I16),
-            pltpu.VMEM(band, I16),
         ]
+        + [pltpu.VMEM(band, jnp.int32)] * 3
         + [pltpu.VMEM((8, LANES), F32)] * 6
         + [
-            pltpu.VMEM((n_mem + 1, 2, local_members, LANES), I16),
-            pltpu.VMEM((n_mem, 2, 2, local_members, LANES), I16),
+            pltpu.VMEM((2, n_mem + 1, 8, LANES), jnp.int32),
+            pltpu.VMEM((n_mem, 2, 2, 8, LANES), jnp.int32),
+            pltpu.VMEM((2, 1, LANES), F32),
+            pltpu.VMEM((n_mem, 2, 1, LANES), F32),
             pltpu.VMEM((1, LANES), F32),
             pltpu.VMEM((n_mem, 1, LANES), F32),
-            pltpu.VMEM(part, F32),
+            pltpu.VMEM(part, jnp.int32),
             pltpu.VMEM(part, BF16),
-            pltpu.VMEM(part, F32),
+            pltpu.VMEM(part, BF16),
+            pltpu.VMEM(part, jnp.int32),
             pltpu.VMEM(part, BF16),
             pltpu.VMEM(part, BF16),
         ]
-        + [pltpu.SemaphoreType.REGULAR, pltpu.SemaphoreType.REGULAR]
+        + [pltpu.SemaphoreType.REGULAR]
         + [dma((4,)), dma((2,)), dma((2,)), dma((4,)), dma((4,))]
-        + [dma((n_mem,))] * 10,
+        + [dma(())] * 12,
         compiler_params=pltpu.CompilerParams(collective_id=0, has_side_effects=True),
     )(
         sample_collection.reshape(flat),

time: 48.8 us -> 44.1 us (0.904)
  Pallas kernels: 48 us -> 43.3 us
    pallas_call x1, Pallas kernels: 48 us -> 43.3 us  [local(): pl.pallas_call(functools.partial(kernel, n_mem, n_rows), out_shape=pltpu....]
where the time goes in v3:
time: 44.1 us; the launch traced here: 44 us
  Pallas kernels  43.3 us (98%)
  local copies, waits for them, and re-layouts  0.66 us (1%)
    pallas_call x1, Pallas kernels, local(): pl.pallas_call(functools.partial(kernel, n_mem, n_rows), out_shape=pltpu....  43.3 us

profile of v3, /device:TPU:2, one launch (start us, length us, event | category | flops | bytes accessed | tf_op | source)
XLA Modules:
  0.0 44.0 jit_solution(5265226031635528426)
XLA Ops:
  0.0 43.3 %shard_map.46 = f32[256,128]{1,0:T(8,128)S(1)} custom-call(f32[256,128]{1,0:T(8,128)} %bitcast.3, f32[2,8,8]{2,1,0:T(8,128)} %values_ref.1, f32[2,8,8]{2,1,0:T(8,128)} %variance_ref.1, s32[2,8,8]{2,1,0:T(8,128)} %mask_ref.1), custom_call_target="tpu_custom_call" | custom-call | tf_op jit(solution)/shard_map/pallas_call | solution.py:423
  43.3 0.7 %copy.6 = f32[16,2,8,128]{3,2,1,0:T(8,128)} copy(f32[16,2,8,128]{3,2,1,0:T(8,128)S(1)} %bitcast.2) | data formatting | bytes 262144

commit v4 on v3

--- a/solution.py
+++ b/solution.py
@@ -150,14 +150,25 @@
     for r in range(PATCH):
         row = tuple(lane_roll(rows_of(x_local, r, f)[...], RADIUS) for f in range(2))
         own_rows.append(row)
-        band[r] = pair_codes(*(value * (LIMIT / BOUND) for value in row))
+        word = pair_codes(*(value * (LIMIT / BOUND) for value in row))
+        for half in range(2):
+            band[half, r] = word[8 * half : 8 * half + 8]
 
     pl.semaphore_wait(barrier, 2 + len(near))
 
-    to_below = remote(band, band_above, band_send.at[0], band_recv.at[0], me_mem, below)
-    to_above = remote(band, band_below, band_send.at[1], band_recv.at[1], me_mem, above)
-    to_below.start()
-    to_above.start()
+    band_copies = [
+        [
+            remote(
+                band.at[half], part.at[half],
+                band_send.at[half, i], band_recv.at[half, i], me_mem, row,
+            )
+            for i, (part, row) in enumerate([(band_above, below), (band_below, above)])
+        ]
+        for half in range(2)
+    ]
+    for copies in band_copies:
+        for copy in copies:
+            copy.start()
     for step in (4, -4):
         greet(token, ring(me_mem, step), me_row)
 
@@ -189,14 +200,14 @@
     obs_copies[0].start()
     obs_copies[1].start()
 
-    to_below.wait_recv()
-    to_above.wait_recv()
 
     def rows_in(part, half):
-        words = [part[r, 8 * half : 8 * half + 8] for r in range(PATCH)]
+        words = [part[half, r] for r in range(PATCH)]
         return [tuple(v * (BOUND / LIMIT) for v in codes_of(word)) for word in words]
 
     for half in range(2):
+        for copy in band_copies[half]:
+            copy.wait_recv()
         rows = rows_in(band_above, half)
         rows += [tuple(v[8 * half : 8 * half + 8] for v in row) for row in own_rows]
         rows += rows_in(band_below, half)
@@ -366,9 +377,7 @@
         ).start()
     own_part[me_mem] = analysed[me_mem]
     back_units[me_mem] = back_unit[...]
-    to_below.wait_send()
-    to_above.wait_send()
-    for copy in obs_copies:
+    for copy in band_copies[0] + band_copies[1] + obs_copies:
         copy.wait_send()
     region_all.wait_send()
     unit_all.wait_send()
@@ -389,6 +398,17 @@
         jnp.concatenate([v * unit_row for v in codes_of(tile)], 0)
         for tile in swap_chunks([own_part[j] for j in range(n_mem)])
     ]
+    state = [{} for _ in range(FSTEPS + 1)]
+    state[0] = {i: (own_tiles[4 + i], own_tiles[(12 + i) % 16]) for i in range(PATCH)}
+
+    def fill(first, last):
+        for step in range(1, FSTEPS + 1):
+            before, after = state[step - 1], state[step]
+            for r in range(first + step, last - step):
+                if r not in after:
+                    after[r] = advance(before[r - 1], before[r], before[r + 1])
+
+    fill(0, PATCH)
     down_all.wait_recv()
     up_all.wait_recv()
     edge_tiles = swap_chunks(
@@ -402,12 +422,13 @@
         pick = slice(8 * part, 8 * part + 8)
         return jnp.concatenate([edge_tiles[first][pick], edge_tiles[second][pick]], 0)
 
-    rows = [(edge_row(1, 8 + i, 4 + i), edge_row(1, i, 12 + i)) for i in range(4)]
-    rows += [(own_tiles[4 + i], own_tiles[(12 + i) % 16]) for i in range(PATCH)]
-    rows += [(edge_row(0, 4 + i, 8 + i), edge_row(0, 12 + i, i)) for i in range(4)]
-    for r, row in enumerate(forecast_rows(rows)):
+    for i in range(RADIUS):
+        state[0][i - RADIUS] = (edge_row(1, 8 + i, 4 + i), edge_row(1, i, 12 + i))
+        state[0][i + PATCH] = (edge_row(0, 4 + i, 8 + i), edge_row(0, 12 + i, i))
+    fill(-RADIUS, PATCH + RADIUS)
+    for r in range(PATCH):
         for f in range(2):
-            rows_of(out_ref, r, f)[...] = row[f]
+            rows_of(out_ref, r, f)[...] = state[FSTEPS][r][f]
 
     for copies in (own_all, back_all, down_all, up_all):
         copies.wait_send()
@@ -417,7 +438,7 @@
     n_mem, n_rows = lax.axis_size("mem"), lax.axis_size("rows")
     local_members = sample_collection.shape[0]
     dma = pltpu.SemaphoreType.DMA
-    band = (PATCH, local_members, LANES)
+    band = (2, PATCH, local_members // 2, LANES)
     flat = (local_members * 2 * PATCH, LANES)
     part = (n_mem, local_members // 2, LANES)
     result = pl.pallas_call(
@@ -448,7 +469,7 @@
             pltpu.VMEM(part, BF16),
         ]
         + [pltpu.SemaphoreType.REGULAR]
-        + [dma((4,)), dma((2,)), dma((2,)), dma((4,)), dma((4,))]
+        + [dma((4,)), dma((2, 2)), dma((2, 2)), dma((4,)), dma((4,))]
         + [dma(())] * 12,
         compiler_params=pltpu.CompilerParams(collective_id=0, has_side_effects=True),
     )(

time: 44.1 us -> 43.8 us (level)
  no operation moved by 1% of the time
where the time goes in v4:
time: 43.8 us; the launch traced here: 43.6 us
  Pallas kernels  43 us (98%)
  local copies, waits for them, and re-layouts  0.66 us (2%)
    pallas_call x1, Pallas kernels, local(): pl.pallas_call(functools.partial(kernel, n_mem, n_rows), out_shape=pltpu....  43 us

profile of v4, /device:TPU:2, one launch (start us, length us, event | category | flops | bytes accessed | tf_op | source)
XLA Modules:
  0.0 43.6 jit_solution(8746126241663455996)
XLA Ops:
  0.0 43.0 %shard_map.46 = f32[256,128]{1,0:T(8,128)S(1)} custom-call(f32[256,128]{1,0:T(8,128)} %bitcast.3, f32[2,8,8]{2,1,0:T(8,128)} %values_ref.1, f32[2,8,8]{2,1,0:T(8,128)} %variance_ref.1, s32[2,8,8]{2,1,0:T(8,128)} %mask_ref.1), custom_call_target="tpu_custom_call" | custom-call | tf_op jit(solution)/shard_map/pallas_call | solution.py:444
  43.0 0.7 %copy.6 = f32[16,2,8,128]{3,2,1,0:T(8,128)} copy(f32[16,2,8,128]{3,2,1,0:T(8,128)S(1)} %bitcast.2) | data formatting | bytes 262144

commit v5 on v4

--- a/solution.py
+++ b/solution.py
@@ -113,21 +113,6 @@
     offsets = sorted(range(1, n_mem), key=lambda d: -min(d, n_mem - d))
     partners = [lax.rem(me_mem + d, n_mem) for d in offsets]
 
-    barrier = pltpu.get_barrier_semaphore()
-
-    def ring(mem, step):
-        return lax.rem(mem + step + n_mem, n_mem)
-
-    def greet(semaphore, mem, row):
-        pl.semaphore_signal(semaphore, inc=1, device_id=at(mem, row), device_id_type=MESH)
-
-    pair = me_mem + 1 - 2 * lax.rem(me_mem, 2)
-    near = [pair] + [ring(mem, step) for mem in (me_mem, pair) for step in (4, -4, 2, -2)]
-    for row in (above, below):
-        greet(barrier, me_mem, row)
-    for mem in near:
-        greet(barrier, mem, me_row)
-
     loads = [
         pltpu.make_async_copy(source, target, load_sem.at[i])
         for i, (source, target) in enumerate(
@@ -139,7 +124,25 @@
             ]
         )
     ]
-    for load in loads:
+    loads[0].start()
+
+    barrier = pltpu.get_barrier_semaphore()
+
+    def ring(mem, step):
+        return lax.rem(mem + step + n_mem, n_mem)
+
+    def greet(semaphore, mem, row):
+        pl.semaphore_signal(semaphore, inc=1, device_id=at(mem, row), device_id_type=MESH)
+
+    pair = me_mem + 1 - 2 * lax.rem(me_mem, 2)
+    near = [pair] + [ring(mem, step) for mem in (me_mem, pair) for step in (4, -4, 2, -2)]
+    distant = [ring(mem, step) for step in (8, 6, -6) for mem in (me_mem, pair)]
+    for row in (above, below):
+        greet(barrier, me_mem, row)
+    for mem in near:
+        greet(barrier, mem, me_row)
+
+    for load in loads[1:]:
         load.start()
     loads[0].wait()
 
@@ -219,14 +222,21 @@
             chunks[half, j] = tiles[j]
         chunks[half, n_mem] = tiles[0]
 
-        if half == 0:
-            pl.semaphore_wait(token, 2)
-
-        for partner in partners:
+        def send(partner):
             remote(
                 chunks.at[half, pl.ds(partner, 2)], regions.at[me_mem, half],
                 region_send, region_recv, partner, me_row,
             ).start()
+
+        if half == 0:
+            for partner in near:
+                send(partner)
+            pl.semaphore_wait(token, 2)
+            for partner in distant:
+                send(partner)
+        else:
+            for partner in partners:
+                send(partner)
     for partner in partners:
         remote(unit, units.at[me_mem], unit_send, unit_recv, partner, me_row).start()
     for half in range(2):

time: 43.8 us -> 43.9 us (level)
  no operation moved by 1% of the time
where the time goes in v5:
time: 43.9 us; the launch traced here: 43.8 us
  Pallas kernels  43.1 us (98%)
  local copies, waits for them, and re-layouts  0.66 us (2%)
    pallas_call x1, Pallas kernels, local(): pl.pallas_call(functools.partial(kernel, n_mem, n_rows), out_shape=pltpu....  43.1 us

profile of v5, /device:TPU:2, one launch (start us, length us, event | category | flops | bytes accessed | tf_op | source)
XLA Modules:
  0.0 43.8 jit_solution(8569883594882953957)
XLA Ops:
  0.0 43.1 %shard_map.46 = f32[256,128]{1,0:T(8,128)S(1)} custom-call(f32[256,128]{1,0:T(8,128)} %bitcast.3, f32[2,8,8]{2,1,0:T(8,128)} %values_ref.1, f32[2,8,8]{2,1,0:T(8,128)} %variance_ref.1, s32[2,8,8]{2,1,0:T(8,128)} %mask_ref.1), custom_call_target="tpu_custom_call" | custom-call | tf_op jit(solution)/shard_map/pallas_call | solution.py:454
  43.1 0.7 %copy.6 = f32[16,2,8,128]{3,2,1,0:T(8,128)} copy(f32[16,2,8,128]{3,2,1,0:T(8,128)S(1)} %bitcast.2) | data formatting | bytes 262144

commit v6 on v5

--- a/solution.py
+++ b/solution.py
@@ -136,7 +136,6 @@
 
     pair = me_mem + 1 - 2 * lax.rem(me_mem, 2)
     near = [pair] + [ring(mem, step) for mem in (me_mem, pair) for step in (4, -4, 2, -2)]
-    distant = [ring(mem, step) for step in (8, 6, -6) for mem in (me_mem, pair)]
     for row in (above, below):
         greet(barrier, me_mem, row)
     for mem in near:
@@ -222,21 +221,14 @@
             chunks[half, j] = tiles[j]
         chunks[half, n_mem] = tiles[0]
 
-        def send(partner):
+        if half == 0:
+            pl.semaphore_wait(token, 2)
+
+        for partner in partners:
             remote(
                 chunks.at[half, pl.ds(partner, 2)], regions.at[me_mem, half],
                 region_send, region_recv, partner, me_row,
             ).start()
-
-        if half == 0:
-            for partner in near:
-                send(partner)
-            pl.semaphore_wait(token, 2)
-            for partner in distant:
-                send(partner)
-        else:
-            for partner in partners:
-                send(partner)
     for partner in partners:
         remote(unit, units.at[me_mem], unit_send, unit_recv, partner, me_row).start()
     for half in range(2):

time: 43.9 us -> 43.8 us (level)
  no operation moved by 1% of the time
where the time goes in v6:
time: 43.8 us; the launch traced here: 43.6 us
  Pallas kernels  43 us (98%)
  local copies, waits for them, and re-layouts  0.66 us (2%)
    pallas_call x1, Pallas kernels, local(): pl.pallas_call(functools.partial(kernel, n_mem, n_rows), out_shape=pltpu....  43 us

profile of v6, /device:TPU:2, one launch (start us, length us, event | category | flops | bytes accessed | tf_op | source)
XLA Modules:
  0.0 43.6 jit_solution(7176303477244933591)
XLA Ops:
  0.0 43.0 %shard_map.46 = f32[256,128]{1,0:T(8,128)S(1)} custom-call(f32[256,128]{1,0:T(8,128)} %bitcast.3, f32[2,8,8]{2,1,0:T(8,128)} %values_ref.1, f32[2,8,8]{2,1,0:T(8,128)} %variance_ref.1, s32[2,8,8]{2,1,0:T(8,128)} %mask_ref.1), custom_call_target="tpu_custom_call" | custom-call | tf_op jit(solution)/shard_map/pallas_call | solution.py:446
  43.0 0.7 %copy.6 = f32[16,2,8,128]{3,2,1,0:T(8,128)} copy(f32[16,2,8,128]{3,2,1,0:T(8,128)S(1)} %bitcast.2) | data formatting | bytes 262144
